TPU v7x, 32 devices: a whole 2x2x4 slice. The times are simulated.
32 devices in a mesh: section: 2 (over core), fsdp: 16 (over z, y, x).
Axes of the slice: x: 2, y: 2, z: 4, core: 2. Of those that a mesh axis runs over, the one named last changes fastest.
Arguments:
- block_input: bfloat16 [4, 16, 7, 14, 512], P(None, 'fsdp'), may hold values from -6 to 6
- cotangent: bfloat16 [4, 16, 7, 14, 512], P(None, 'fsdp'), may hold values from -6 to 6
- qkv_weight: bfloat16 [2, 512, 1536], P('section', 'fsdp'), may hold values from -0.25 to 0.25
- proj_weight: bfloat16 [2, 512, 512], P('section', 'fsdp'), may hold values from -2 to 2
- fc1_weight: bfloat16 [2, 512, 2048], P('section', 'fsdp'), may hold values from -0.25 to 0.25
- fc2_weight: bfloat16 [2, 2048, 512], P('section', 'fsdp'), may hold values from -0.125 to 0.125
- vectors: bfloat16 [2, 6144], P('section', 'fsdp'), may hold values from -2 to 2, as said below
- rel_table: float32 [2, 169, 16], P('section'), may hold values from -4 to 4
Outputs:
- layer_outputs: bfloat16 [2, 4, 16, 7, 14, 512], P('section', None, 'fsdp')
- input_grads: float32 [2, 4, 16, 7, 14, 512], P('section', None, 'fsdp')
- qkv_grad: float32 [2, 512, 1536], P('section', 'fsdp')
- proj_grad: float32 [2, 512, 512], P('section', 'fsdp')
- fc1_grad: float32 [2, 512, 2048], P('section', 'fsdp')
- fc2_grad: float32 [2, 2048, 512], P('section', 'fsdp')
- vectors_grad: float32 [2, 6144], P('section', 'fsdp')
- table_grad: float32 [2, 169, 16], P('section')
Inputs may be any that keep to these rules, and one draw needn't show every extreme that they name: `vectors`: entries 0 to 511 and 2560 to 3071 of each row lie in 0.5 to 1.5.
All inputs are finite; a program needn't handle non-finite values.
Results may differ from a plain program's by a relative error of at most 0.015.
The roundings to bfloat16 on the way count: a program that leaves them out, or rounds other values in their place, can miss the bound.
Values may be sent and summed in bfloat16 or wider, within the bound.
A program may use at most 192 MiB of HBM per device.

v0:
```python
import jax
import jax.numpy as jnp
from jax import lax
from jax.sharding import PartitionSpec as P

D = 512
FF = 2048
H = 16
HD = 32
WIN = 7
SHIFT = 3
SIDE = 14
TABLE_ROWS = 169


EPS = 1e-05


def partner(x, axis, apart):
    return lax.ppermute(x, axis, [(i, i ^ 1 << apart) for i in range(lax.axis_size(axis))])


def from_behind(value, axis, steps):
    count = lax.axis_size(axis)
    leading, last = (max(0, -steps), min(count, count - steps))
    return lax.ppermute(value, axis, [(source, source + steps) for source in range(leading, last)])


def plain_product(first, second):
    return jnp.dot(first, second, preferred_element_type=jnp.float32)


def left_product(first, second):
    return lax.dot_general(
        first, second, (((0,), (0,)), ((), ())), preferred_element_type=jnp.float32
    )


def right_product(first, second):
    return lax.dot_general(
        first, second, (((1,), (1,)), ((), ())), preferred_element_type=jnp.float32
    )


def batched(form, first, second):
    return jnp.einsum(form, first, second, preferred_element_type=jnp.float32)


def layer_norm(values, gain, offset):
    average = jnp.mean(values, -1, keepdims=True)
    centred = values - average
    spread = jnp.mean(centred * centred, -1, keepdims=True)
    return centred * lax.rsqrt(spread + EPS) * gain + offset


def to_windows(grid):
    batch, rows, cols, width = grid.shape
    grid = grid.reshape(batch, rows // WIN, WIN, cols // WIN, WIN, width)
    return grid.transpose(0, 1, 3, 2, 4, 5).reshape(-1, WIN * WIN, width)


def from_windows(tokens, batch, rows, cols):
    width = tokens.shape[-1]
    tokens = tokens.reshape(batch, rows // WIN, cols // WIN, WIN, WIN, width)
    return tokens.transpose(0, 1, 3, 2, 4, 5).reshape(batch, rows, cols, width)


def region(position):
    return (position >= SIDE - WIN).astype(jnp.int32) + (position >= SIDE - SHIFT).astype(jnp.int32)


def allowed_pairs(row_start, rows, shifted_flag):
    row_index = row_start + jnp.arange(rows, dtype=jnp.int32)
    labels = region(row_index)[:, None] * 3 + region(jnp.arange(SIDE, dtype=jnp.int32))[None, :]
    labels = labels[None, :, :, None]
    windowed = to_windows(labels)[:, :, 0]
    same = windowed[:, :, None] == windowed[:, None, :]
    return same | jnp.logical_not(shifted_flag)


def relative_onehot():
    positions = jnp.arange(WIN * WIN, dtype=jnp.int32)
    prow = positions // WIN
    pcol = positions % WIN
    offset = (
        (prow[:, None] - prow[None, :] + WIN - 1) * (2 * WIN - 1)
        + pcol[:, None]
        - pcol[None, :]
        + WIN
        - 1
    )
    return (offset.reshape(-1)[:, None] == jnp.arange(TABLE_ROWS, dtype=jnp.int32)[None, :]).astype(
        jnp.float32
    )


def split_vectors(vector_row):
    values = vector_row.astype(jnp.float32)
    pieces = []
    start = 0
    for extent in [D] * 7 + [FF, D]:
        pieces.append(values[start : start + extent])
        start = start + extent
    return pieces


def recompute(grid_b, weights, vector_row, table, allowed, onehot):
    w_qkv, w_proj, w_up, w_down = weights
    parts = split_vectors(vector_row)
    base = to_windows(grid_b.astype(jnp.float32)).reshape(-1, D)
    normed = layer_norm(base, parts[0], parts[1]).astype(jnp.bfloat16)
    table_bias = jnp.dot(onehot, table, precision=lax.Precision.HIGHEST)
    table_bias = table_bias.reshape(WIN * WIN, WIN * WIN, H).transpose(2, 0, 1)
    mixed = plain_product(normed, w_qkv)
    scale = HD ** (-0.5)
    query = ((mixed[:, :D] + parts[2]) * scale).astype(jnp.bfloat16).reshape(-1, WIN * WIN, H, HD)
    keys = mixed[:, D : 2 * D].astype(jnp.bfloat16).reshape(-1, WIN * WIN, H, HD)
    values = (mixed[:, 2 * D :] + parts[3]).astype(jnp.bfloat16).reshape(-1, WIN * WIN, H, HD)
    scores = batched("wihd,wjhd->whij", query, keys) + table_bias[None]
    scores = jnp.where(allowed[:, None], scores, -jnp.inf)
    highest = jnp.max(scores, -1, keepdims=True)
    expo = jnp.exp(scores - highest)
    soft = expo / jnp.sum(expo, -1, keepdims=True)
    attended = (
        batched("whij,wjhd->wihd", soft.astype(jnp.bfloat16), values)
        .astype(jnp.bfloat16)
        .reshape(-1, D)
    )
    middle = base + plain_product(attended, w_proj) + parts[4]
    second = layer_norm(middle, parts[5], parts[6]).astype(jnp.bfloat16)
    upward = plain_product(second, w_up) + parts[7]
    activated = jax.nn.gelu(upward, approximate=False).astype(jnp.bfloat16)
    result = middle + plain_product(activated, w_down) + parts[8]
    saved = (
        parts,
        base,
        normed,
        query,
        keys,
        values,
        soft,
        attended,
        middle,
        second,
        upward,
        activated,
    )
    return (result, saved)


def block_forward(grid_b, weights, vector_row, table, allowed, onehot):
    batch, rows, cols, _ = grid_b.shape
    result, _ = recompute(grid_b, weights, vector_row, table, allowed, onehot)
    return from_windows(result.reshape(-1, WIN * WIN, D), batch, rows, cols)


def block_backward(grid_b, grad_grid, weights, vector_row, table, allowed, onehot):
    batch, rows, cols, _ = grid_b.shape
    w_qkv, w_proj, w_up, w_down = weights
    _, saved = recompute(grid_b, weights, vector_row, table, allowed, onehot)
    parts, base, normed, query, keys, values, soft, attended, middle, second, upward, activated = (
        saved
    )
    grad_out = to_windows(grad_grid).reshape(-1, D)
    down_in = grad_out.astype(jnp.bfloat16)
    grad_down = left_product(activated, down_in)
    grad_act = right_product(down_in, w_down)
    _, gelu_back = jax.vjp(lambda inner: jax.nn.gelu(inner, approximate=False), upward)
    grad_up = gelu_back(grad_act)[0]
    up_in = grad_up.astype(jnp.bfloat16)
    grad_upw = left_product(second, up_in)
    grad_second = right_product(up_in, w_up)
    _, second_back = jax.vjp(layer_norm, middle, parts[5], parts[6])
    grad_mid_norm, grad_gain2, grad_bias2 = second_back(grad_second)
    grad_mid = grad_out + grad_mid_norm
    proj_in = grad_mid.astype(jnp.bfloat16)
    grad_proj = left_product(attended, proj_in)
    grad_att = right_product(proj_in, w_proj).astype(jnp.bfloat16).reshape(-1, WIN * WIN, H, HD)
    grad_soft = batched("wihd,wjhd->whij", grad_att, values)
    grad_values = batched("whij,wihd->wjhd", soft.astype(jnp.bfloat16), grad_att)
    grad_scores = soft * (grad_soft - jnp.sum(soft * grad_soft, -1, keepdims=True))
    pair_sums = jnp.sum(grad_scores, 0).transpose(1, 2, 0).reshape(-1, grad_scores.shape[1])
    grad_table = lax.dot_general(
        onehot, pair_sums, (((0,), (0,)), ((), ())), precision=lax.Precision.HIGHEST
    )
    scores_b = grad_scores.astype(jnp.bfloat16)
    grad_query = (batched("whij,wjhd->wihd", scores_b, keys) * HD ** (-0.5)).reshape(-1, D)
    grad_keys = batched("whij,wihd->wjhd", scores_b, query).reshape(-1, D)
    grad_values = grad_values.reshape(-1, D)
    mixed_in = jnp.concatenate([grad_query, grad_keys, grad_values], 1).astype(jnp.bfloat16)
    grad_qkv = left_product(normed, mixed_in)
    grad_normed = right_product(mixed_in, w_qkv)
    _, first_back = jax.vjp(layer_norm, base, parts[0], parts[1])
    grad_base_norm, grad_gain1, grad_bias1 = first_back(grad_normed)
    grad_base = grad_mid + grad_base_norm
    grad_vectors = jnp.concatenate(
        [
            grad_gain1,
            grad_bias1,
            jnp.sum(grad_query, 0),
            jnp.sum(grad_values, 0),
            jnp.sum(grad_mid, 0),
            grad_gain2,
            grad_bias2,
            jnp.sum(grad_up, 0),
            jnp.sum(grad_out, 0),
        ]
    )
    grid_out = from_windows(grad_base.reshape(-1, WIN * WIN, D), batch, rows, cols)
    return (grid_out, (grad_qkv, grad_proj, grad_upw, grad_down, grad_vectors), grad_table)


def strip_swap(strip):
    return partner(strip, "fsdp", 0)


def grad_swap(strip):
    return partner(strip.astype(jnp.bfloat16), "fsdp", 0).astype(strip.dtype)


def roll_rows_in(grid, swapper):
    strip = swapper(grid[:, :SHIFT])
    rows = jnp.concatenate([grid[:, SHIFT:], strip], 1)
    return jnp.roll(rows, -SHIFT, 2)


def roll_rows_out(grid, swapper):
    strip = swapper(grid[:, WIN - SHIFT :])
    rows = jnp.concatenate([strip, grid[:, : WIN - SHIFT]], 1)
    return jnp.roll(rows, SHIFT, 2)


def on_device(
    block_input, cotangent, qkv_weight, proj_weight, fc1_weight, fc2_weight, vectors, rel_table
):
    section = lax.axis_index("section")
    shifted = section == 1
    onehot = relative_onehot()
    allowed = allowed_pairs(lax.axis_index("fsdp") % 2 * WIN, WIN, shifted)
    shards = (qkv_weight[0], proj_weight[0], fc1_weight[0], fc2_weight[0], vectors[0])
    gathered = (
        lax.all_gather(shards[0], "fsdp", axis=0, tiled=True),
        lax.all_gather(shards[1], "fsdp", axis=0, tiled=True),
        lax.all_gather(shards[2], "fsdp", axis=0, tiled=True),
        lax.all_gather(shards[3], "fsdp", axis=0, tiled=True),
        lax.all_gather(shards[4], "fsdp", axis=0, tiled=True),
    )
    weights = gathered[:4]
    vector_row = gathered[4]
    table = rel_table[0]
    count = block_input.shape[0]
    kept = jnp.zeros(block_input.shape, jnp.bfloat16)
    produced = jnp.zeros(block_input.shape, jnp.bfloat16)
    incoming = jnp.zeros(block_input.shape[1:], jnp.bfloat16)
    for tick in range(count + 1):
        micro = tick - section
        valid = (micro >= 0) & (micro < count)
        place = jnp.clip(micro, 0, count - 1)
        source = jnp.where(section == 0, block_input[min(tick, count - 1)], incoming)
        rolled = jnp.where(shifted, roll_rows_in(source, strip_swap), source)
        result = block_forward(rolled, weights, vector_row, table, allowed, onehot).astype(
            jnp.bfloat16
        )
        output = jnp.where(shifted, roll_rows_out(result, strip_swap), result)
        kept = jnp.where(valid, kept.at[place].set(rolled), kept)
        produced = jnp.where(valid, produced.at[place].set(output), produced)
        if tick < count:
            incoming = from_behind(output, "section", 1)
    sums = tuple((jnp.zeros(piece.shape, jnp.float32) for piece in gathered))
    table_sum = jnp.zeros(table.shape, jnp.float32)
    returned = jnp.zeros(block_input.shape, jnp.float32)
    incoming_grad = jnp.zeros(block_input.shape[1:], jnp.float32)
    for tick in range(count + 1):
        micro = tick - 1 + section
        valid = (micro >= 0) & (micro < count)
        place = jnp.clip(micro, 0, count - 1)
        arriving = jnp.where(
            section == 1, cotangent[min(tick, count - 1)].astype(jnp.float32), incoming_grad
        )
        grad_in = jnp.where(shifted, roll_rows_in(arriving, grad_swap), arriving)
        grad_grid, grads, grad_table = block_backward(
            kept[place], grad_in, weights, vector_row, table, allowed, onehot
        )
        grad_source = jnp.where(shifted, roll_rows_out(grad_grid, grad_swap), grad_grid)
        sums = tuple((jnp.where(valid, total + part, total) for total, part in zip(sums, grads)))
        table_sum = jnp.where(valid, table_sum + grad_table, table_sum)
        returned = jnp.where(valid, returned.at[place].set(grad_source), returned)
        if tick < count:
            incoming_grad = from_behind(grad_source.astype(jnp.bfloat16), "section", -1).astype(
                grad_source.dtype
            )
    scattered = (
        lax.psum_scatter(sums[0], "fsdp", scatter_dimension=0, tiled=True),
        lax.psum_scatter(sums[1], "fsdp", scatter_dimension=0, tiled=True),
        lax.psum_scatter(sums[2], "fsdp", scatter_dimension=0, tiled=True),
        lax.psum_scatter(sums[3], "fsdp", scatter_dimension=0, tiled=True),
        lax.psum_scatter(sums[4], "fsdp", scatter_dimension=0, tiled=True),
    )
    table_total = lax.psum(table_sum, "fsdp")
    return (
        produced[None],
        returned[None],
        scattered[0][None],
        scattered[1][None],
        scattered[2][None],
        scattered[3][None],
        scattered[4][None],
        table_total[None],
    )


def solution(mesh):
    in_specs = (
        P(None, "fsdp", None, None, None),
        P(None, "fsdp", None, None, None),
        P("section", "fsdp", None),
        P("section", "fsdp", None),
        P("section", "fsdp", None),
        P("section", "fsdp", None),
        P("section", "fsdp"),
        P("section", None, None),
    )
    out_specs = (
        P("section", None, "fsdp", None, None, None),
        P("section", None, "fsdp", None, None, None),
        P("section", "fsdp", None),
        P("section", "fsdp", None),
        P("section", "fsdp", None),
        P("section", "fsdp", None),
        P("section", "fsdp"),
        P("section", None, None),
    )
    return jax.shard_map(
        on_device, mesh=mesh, in_specs=in_specs, out_specs=out_specs, check_vma=False
    )
```

profile of v0, /device:TPU:0, one launch (start us, length us, event | category | flops | bytes accessed | tf_op | source)
XLA Modules:
  0.0 1158.3 jit_solution(12706647054403028019)
XLA Ops:
  15.1 40.4 %all-gather = bf16[1,6144]{1,0:T(2,128)(2,1)S(1)} all-gather(bf16[1,384]{1,0:T(2,128)(2,1)S(1)} %copy-done.297), channel_id=2, replica_groups=mesh['section'=2,'fsdp'=16] {'fsdp'}, dimensions={1}, use_global_device_ids=true | all-gather | bytes 13056 | tf_op jit(solution)/shard_map/all_gather | solution.py:246
  57.7 39.6 %all-gather.2 = bf16[1,512,512]{2,1,0:T(8,128)(2,1)S(1)} all-gather(bf16[1,32,512]{2,1,0:T(8,128)(2,1)S(1)} %copy-done.218), channel_id=4, replica_groups=mesh['section'=2,'fsdp'=16] {'fsdp'}, dimensions={1}, use_global_device_ids=true | all-gather | bytes 557056 | tf_op jit(solution)/shard_map/all_gather | solution.py:243
  106.4 28.7 %all-gather.13.cloned.1.call-done = bf16[1,2048,512]{2,1,0:T(8,128)(2,1)} async-done(((bf16[1,128,512]{2,1,0:T(8,128)(2,1)}), bf16[1,2048,512]{2,1,0:T(8,128)(2,1)}) %all-gather.13.cloned.1.call-update) | async-done | bytes 2097168 | tf_op jit(solution)/shard_map/all_gather | solution.py:245
  135.1 62.0 %all-gather.11.cloned.1.call-done = bf16[1,512,2048]{2,1,0:T(8,128)(2,1)} async-done(((bf16[1,32,2048]{2,1,0:T(8,128)(2,1)}), bf16[1,512,2048]{2,1,0:T(8,128)(2,1)}) %all-gather.11.cloned.1.call-update) | async-done | bytes 2097168 | tf_op jit(solution)/shard_map/all_gather | solution.py:244
  197.1 4.7 fusion.199
  234.5 5.4 fusion.196
  274.1 5.4 fusion.193
  320.6 4.8 fusion.190
  556.6 4.9 fusion.965
  575.0 3.3 fusion.931
  614.0 4.9 fusion.964
  632.4 3.2 fusion.933
  673.8 4.9 fusion.963
  692.3 3.4 fusion.935
  735.1 4.9 fusion.962
  761.9 3.3 fusion.937
  772.5 4.5 add_select_fusion.8
  782.7 3.6 add_select_fusion.4
  808.7 4.8 fusion.187
  826.8 3.5 fusion.357
  837.3 4.7 add_select_fusion
  898.9 76.5 %all-reduce.1 = (f32[6144]{0:T(1024)S(1)}, f32[1,169,16]{1,2,0:T(8,128)}) all-reduce(f32[6144]{0:T(1024)S(1)} %add_select_fusion.16, f32[1,169,16]{1,2,0:T(8,128)S(1)} %fusion.211), channel_id=11, replica_groups=mesh['section'=2,'fsdp'=16] {'fsdp'}, use_global_device_ids=true, to_apply=%region_144.145.clone | all-reduce | flops 8848 | bytes 70784
  978.6 75.0 %reduce-scatter.9.cloned.1.call-done = f32[32,2048]{1,0:T(8,128)} async-done(((f32[512,2048]{1,0:T(8,128)}), f32[32,2048]{1,0:T(8,128)}) %reduce-scatter.9.cloned.1.call-update) | async-done | bytes 262160 | tf_op jit(solution)/shard_map/reduce_scatter | solution.py:295
  1053.5 97.7 %reduce-scatter.11.cloned.1.call-done = f32[128,512]{1,0:T(8,128)} async-done(((f32[2048,512]{1,0:T(8,128)}), f32[128,512]{1,0:T(8,128)}) %reduce-scatter.11.cloned.1.call-update) | async-done | bytes 262160 | tf_op jit(solution)/shard_map/reduce_scatter | solution.py:296
  (1426 shorter events, 644.3 us)
Async XLA Ops:
  7.2 92.1 %all-gather.9.cloned.1.call-start = ((), (), s32[]{:S(2)}) async-start(), calls=%async_computation.8 | async-start | bytes 1671168 | tf_op jit(solution)/shard_map/all_gather | solution.py:242
  7.9 127.2 %all-gather.13.cloned.1.call-start = ((), (), s32[]{:S(2)}) async-start(), calls=%async_computation.10 | async-start | bytes 2228224 | tf_op jit(solution)/shard_map/all_gather | solution.py:245
  8.7 188.4 %all-gather.11.cloned.1.call-start = ((), (), s32[]{:S(2)}) async-start(), calls=%async_computation.9 | async-start | bytes 2228224 | tf_op jit(solution)/shard_map/all_gather | solution.py:244
  11.8 86.0 %collective-permute-start = (bf16[1,3,14,512]{3,1,2,0:T(4,128)(2,1)S(1)}, bf16[1,3,14,512]{3,1,2,0:T(4,128)(2,1)S(1)}, u32[]{:S(2)}, u32[]{:S(2)}) collective-permute-start(bf16[1,3,14,512]{3,1,2,0:T(4,128)(2,1)S(1)} %slice.1059), channel_id=1, source_target_pairs={{0,1},{1,0},{2,3},{3,2},{4,5},{5,4},{6,7},{7,6},{8,9},{9,8},{10,11... | collective-permute-start | bytes 129032 | tf_op jit(solution)/shard_map/ppermute | solution.py:20
  14.9 963.7 %reduce-scatter.7.cloned.1.call-start = ((), (), s32[]{:S(2)}) async-start(), calls=%async_computation.5 | async-start | bytes 1114112 | tf_op jit(solution)/shard_map/reduce_scatter | solution.py:294
  202.0 4.2 collective-permute-start.1
  208.8 4.2 collective-permute-start.3
  240.9 4.5 collective-permute-start.4
  243.7 6.5 collective-permute-start.14
  246.2 4.9 collective-permute-start.5
  252.2 4.2 collective-permute-start.6
  289.5 4.7 collective-permute-start.9
  327.2 4.2 collective-permute-start.10
  335.0 4.2 collective-permute-start.12
  442.0 103.0 %collective-permute-start.15 = (bf16[1,3,14,512]{3,1,2,0:T(4,128)(2,1)}, bf16[1,3,14,512]{3,1,2,0:T(4,128)(2,1)}, u32[]{:S(2)}, u32[]{:S(2)}) collective-permute-start(bf16[1,3,14,512]{3,1,2,0:T(4,128)(2,1)} %slice.1335), channel_id=1, source_target_pairs={{0,1},{1,0},{2,3},{3,2},{4,5},{5,4},{6,7},{7,6},{8,9},{9,8},{10,11... | collective-permute-start | bytes 129032 | tf_op jit(solution)/shard_map/ppermute | solution.py:20
  607.9 4.6 collective-permute-start.20
  665.9 4.6 collective-permute-start.23
  722.8 4.4 collective-permute-start.25
  727.2 4.7 collective-permute-start.26
  744.4 234.2 %reduce-scatter.5.cloned.1.call-start = ((), (), s32[]{:S(2)}) async-start(), calls=%async_computation.4 | async-start | bytes 3342336 | tf_op jit(solution)/shard_map/reduce_scatter | solution.py:293
  777.0 276.5 %reduce-scatter.9.cloned.1.call-start = ((), (), s32[]{:S(2)}) async-start(), calls=%async_computation.6 | async-start | bytes 4456448 | tf_op jit(solution)/shard_map/reduce_scatter | solution.py:295
  786.4 364.8 %reduce-scatter.11.cloned.1.call-start = ((), (), s32[]{:S(2)}) async-start(), calls=%async_computation.7 | async-start | bytes 4456448 | tf_op jit(solution)/shard_map/reduce_scatter | solution.py:296
  814.4 31.0 %collective-permute-start.13 = (bf16[1,3,14,512]{3,1,2,0:T(4,128)(2,1)}, bf16[1,3,14,512]{3,1,2,0:T(4,128)(2,1)S(1)}, u32[]{:S(2)}, u32[]{:S(2)}) collective-permute-start(bf16[1,3,14,512]{3,1,2,0:T(4,128)(2,1)} %slice.1110), channel_id=1, source_target_pairs={{0,1},{1,0},{2,3},{3,2},{4,5},{5,4},{6,7},{7,6},{8,9},{9,8},{10,11... | collective-permute-start | bytes 129032 | tf_op jit(solution)/shard_map/ppermute | solution.py:20
  894.8 81.3 %collective-permute-start.27 = (bf16[1,3,14,512]{3,1,2,0:T(4,128)(2,1)S(1)}, bf16[1,3,14,512]{3,1,2,0:T(4,128)(2,1)S(1)}, u32[]{:S(2)}, u32[]{:S(2)}) collective-permute-start(bf16[1,3,14,512]{3,1,2,0:T(4,128)(2,1)S(1)} %slice.1327), channel_id=1, source_target_pairs={{0,1},{1,0},{2,3},{3,2},{4,5},{5,4},{6,7},{7,6},{8,9},{9,8},{10,11... | collective-permute-start | bytes 129032 | tf_op jit(solution)/shard_map/ppermute | solution.py:20
  (327 other events, 4021.1 us)
Sparse Core Ops, SparseCore 0:
  10.8 62.0 all-gather.8
  75.7 59.3 all-gather.12
  137.9 59.1 all-gather.10
  744.5 77.8 reduce-scatter.6
  827.8 128.7 reduce-scatter.4
  959.3 94.2 reduce-scatter.8
  1056.4 94.7 reduce-scatter.10
where the time goes:
time: 1170 us; the launch traced here: 1160 us
  local copies, waits for them, and re-layouts  354 us (30%)
  waiting for transfers between devices  287 us (25%)
  matrix products  229 us (20%)
  blocking collectives  156 us (13%)
  other arithmetic  72.6 us (6%)
  starting transfers between devices  39.2 us (3%)
  between operations  20 us (2%)
    reduce_scatter x1, waiting for transfers between devices, on_device(): lax.psum_scatter(sums[3], 'fsdp', scatter_dimension=0, tiled=True)  97.7 us
    dot_general x40, matrix products, batched(): return jnp.einsum(form, first, second, preferred_element_type=jnp.float32)  77.6 us
    unnamed x688, local copies, waits for them, and re-layouts  77.3 us
    unnamed x1, blocking collectives  76.5 us
    reduce_scatter x1, waiting for transfers between devices, on_device(): lax.psum_scatter(sums[2], 'fsdp', scatter_dimension=0, tiled=True)  75 us
    all_gather x1, waiting for transfers between devices, on_device(): lax.all_gather(shards[2], 'fsdp', axis=0, tiled=True)  62 us
    dot_general x30, matrix products, plain_product(): return jnp.dot(first, second, preferred_element_type=jnp.float32)  49.8 us
    dot_general x20, matrix products, right_product(): lax.dot_general(first, second, (((1,), (1,)), ((), ())), preferred_elemen...  45.4 us
  transfers between devices with their start and end apart: 35, of which 22 were waited for; matrix products, arithmetic and copies ran while one was open for 25% of the time, Pallas kernels for 0%

commit v1 on v0

--- a/solution.py
+++ b/solution.py
@@ -1,6 +1,8 @@
 import jax
 import jax.numpy as jnp
 from jax import lax
+from jax.experimental import pallas as pl
+from jax.experimental.pallas import tpu as pltpu
 from jax.sharding import PartitionSpec as P
 
 D = 512
@@ -20,12 +22,6 @@
     return lax.ppermute(x, axis, [(i, i ^ 1 << apart) for i in range(lax.axis_size(axis))])
 
 
-def from_behind(value, axis, steps):
-    count = lax.axis_size(axis)
-    leading, last = (max(0, -steps), min(count, count - steps))
-    return lax.ppermute(value, axis, [(source, source + steps) for source in range(leading, last)])
-
-
 def plain_product(first, second):
     return jnp.dot(first, second, preferred_element_type=jnp.float32)
 
@@ -69,13 +65,11 @@
     return (position >= SIDE - WIN).astype(jnp.int32) + (position >= SIDE - SHIFT).astype(jnp.int32)
 
 
-def allowed_pairs(row_start, rows, shifted_flag):
-    row_index = row_start + jnp.arange(rows, dtype=jnp.int32)
-    labels = region(row_index)[:, None] * 3 + region(jnp.arange(SIDE, dtype=jnp.int32))[None, :]
-    labels = labels[None, :, :, None]
-    windowed = to_windows(labels)[:, :, 0]
-    same = windowed[:, :, None] == windowed[:, None, :]
-    return same | jnp.logical_not(shifted_flag)
+def allowed_pairs():
+    index = jnp.arange(SIDE, dtype=jnp.int32)
+    labels = region(index)[:, None] * 3 + region(index)[None, :]
+    windowed = to_windows(labels[None, :, :, None])[:, :, 0]
+    return windowed[:, :, None] == windowed[:, None, :]
 
 
 def relative_onehot():
@@ -117,7 +111,11 @@
     keys = mixed[:, D : 2 * D].astype(jnp.bfloat16).reshape(-1, WIN * WIN, H, HD)
     values = (mixed[:, 2 * D :] + parts[3]).astype(jnp.bfloat16).reshape(-1, WIN * WIN, H, HD)
     scores = batched("wihd,wjhd->whij", query, keys) + table_bias[None]
-    scores = jnp.where(allowed[:, None], scores, -jnp.inf)
+    if allowed is not None:
+        windows = allowed.shape[0]
+        scores = scores.reshape((-1, windows) + scores.shape[1:])
+        scores = jnp.where(allowed[None, :, None], scores, -jnp.inf)
+        scores = scores.reshape((-1,) + scores.shape[2:])
     highest = jnp.max(scores, -1, keepdims=True)
     expo = jnp.exp(scores - highest)
     soft = expo / jnp.sum(expo, -1, keepdims=True)
@@ -148,16 +146,9 @@
     return (result, saved)
 
 
-def block_forward(grid_b, weights, vector_row, table, allowed, onehot):
-    batch, rows, cols, _ = grid_b.shape
-    result, _ = recompute(grid_b, weights, vector_row, table, allowed, onehot)
-    return from_windows(result.reshape(-1, WIN * WIN, D), batch, rows, cols)
-
-
-def block_backward(grid_b, grad_grid, weights, vector_row, table, allowed, onehot):
-    batch, rows, cols, _ = grid_b.shape
+def block_backward(saved, grad_grid, weights, onehot):
+    batch, rows, cols, _ = grad_grid.shape
     w_qkv, w_proj, w_up, w_down = weights
-    _, saved = recompute(grid_b, weights, vector_row, table, allowed, onehot)
     parts, base, normed, query, keys, values, soft, attended, middle, second, upward, activated = (
         saved
     )
@@ -210,101 +201,362 @@
     return (grid_out, (grad_qkv, grad_proj, grad_upw, grad_down, grad_vectors), grad_table)
 
 
-def strip_swap(strip):
-    return partner(strip, "fsdp", 0)
-
-
-def grad_swap(strip):
-    return partner(strip.astype(jnp.bfloat16), "fsdp", 0).astype(strip.dtype)
-
-
-def roll_rows_in(grid, swapper):
-    strip = swapper(grid[:, :SHIFT])
-    rows = jnp.concatenate([grid[:, SHIFT:], strip], 1)
-    return jnp.roll(rows, -SHIFT, 2)
-
-
-def roll_rows_out(grid, swapper):
-    strip = swapper(grid[:, WIN - SHIFT :])
-    rows = jnp.concatenate([strip, grid[:, : WIN - SHIFT]], 1)
-    return jnp.roll(rows, SHIFT, 2)
+MESH_IDS = pl.DeviceIdType.MESH
+
+
+def ring_place(index, count):
+    depth = count // 4
+    layer = index // 4
+    col = index % 4
+    upper = col // 2
+    rank = upper * 2 + (col % 2 + upper) % 2
+    return rank * depth + layer + (rank % 2) * (depth - 1 - 2 * layer)
+
+
+def ring_index(place, count):
+    depth = count // 4
+    place = (place + count) % count
+    rank = place // depth
+    rest = place % depth
+    layer = rest + (rank % 2) * (depth - 1 - 2 * rest)
+    upper = rank // 2
+    return layer * 4 + upper * 2 + (rank % 2 + upper) % 2
+
+
+def enter(section, me, ahead, behind):
+    barrier = pltpu.get_barrier_semaphore()
+    for target in ((section, ahead), (section, behind), (1 - section, me)):
+        pl.semaphore_signal(barrier, inc=1, device_id=target, device_id_type=MESH_IDS)
+    pl.semaphore_wait(barrier, 3)
+
+
+def remote(src, dst, send, recv, target):
+    return pltpu.make_async_remote_copy(
+        src_ref=src,
+        dst_ref=dst,
+        send_sem=send,
+        recv_sem=recv,
+        device_id=target,
+        device_id_type=MESH_IDS,
+    )
+
+
+def gather_kernel(count, own, whole, local_sem, up_s, up_r, down_s, down_r, side_s, side_r):
+    section = lax.axis_index("section")
+    me = lax.axis_index("fsdp")
+    place = ring_place(me, count)
+    ahead = ring_index(place + 1, count)
+    behind = ring_index(place - 1, count)
+    ups = count // 2
+    downs = count - 1 - ups
+    keep = pltpu.make_async_copy(own, whole.at[section, me], local_sem)
+    keep.start()
+    enter(section, me, ahead, behind)
+    sides = []
+
+    def up_copy(step):
+        block = ring_index(place - step, count)
+        piece = own if step == 0 else whole.at[section, block]
+        return remote(
+            piece, whole.at[section, block], up_s.at[step], up_r.at[step], (section, ahead)
+        )
+
+    def down_copy(step):
+        block = ring_index(place + step, count)
+        piece = own if step == 0 else whole.at[section, block]
+        return remote(
+            piece, whole.at[section, block], down_s.at[step], down_r.at[step], (section, behind)
+        )
+
+    def side_copy(block, piece, slot):
+        return remote(
+            piece, whole.at[section, block], side_s.at[slot], side_r.at[slot], (1 - section, me)
+        )
+
+    going = []
+    for step in range(ups):
+        up = up_copy(step)
+        up.start()
+        going.append(up)
+        if step < downs:
+            down = down_copy(step)
+            down.start()
+            going.append(down)
+        if step == 0:
+            side = side_copy(me, own, 0)
+            side.start()
+            sides.append(side)
+        up.wait_recv()
+        block = ring_index(place - step - 1, count)
+        side = side_copy(block, whole.at[section, block], 1 + step)
+        side.start()
+        sides.append(side)
+        if step < downs:
+            down.wait_recv()
+            block = ring_index(place + step + 1, count)
+            side = side_copy(block, whole.at[section, block], 1 + ups + step)
+            side.start()
+            sides.append(side)
+    for copy in going:
+        copy.wait_send()
+    for copy in sides:
+        copy.wait()
+    keep.wait()
+
+
+def gather_all(own, sections, count):
+    ups = count // 2
+    return pl.pallas_call(
+        lambda *refs: gather_kernel(count, *refs),
+        out_shape=jax.ShapeDtypeStruct((sections, count) + own.shape, own.dtype),
+        in_specs=[pl.BlockSpec(memory_space=pl.ANY)],
+        out_specs=pl.BlockSpec(memory_space=pl.ANY),
+        scratch_shapes=[
+            pltpu.SemaphoreType.DMA,
+            pltpu.SemaphoreType.DMA((ups,)),
+            pltpu.SemaphoreType.DMA((ups,)),
+            pltpu.SemaphoreType.DMA((ups,)),
+            pltpu.SemaphoreType.DMA((ups,)),
+            pltpu.SemaphoreType.DMA((count,)),
+            pltpu.SemaphoreType.DMA((count,)),
+        ],
+        compiler_params=pltpu.CompilerParams(collective_id=0, has_side_effects=True),
+        name="gather_weights",
+    )(own)
+
+
+def scatter_kernel(
+    count,
+    parts,
+    out,
+    mine,
+    theirs,
+    first,
+    up_buf,
+    down_buf,
+    local_sem,
+    up_s,
+    up_r,
+    down_s,
+    down_r,
+    side_s,
+    side_r,
+):
+    section = lax.axis_index("section")
+    me = lax.axis_index("fsdp")
+    place = ring_place(me, count)
+    ahead = ring_index(place + 1, count)
+    behind = ring_index(place - 1, count)
+    ups = count // 2
+    downs = count - 1 - ups
+    keep = pltpu.make_async_copy(parts.at[section], mine, local_sem)
+    keep.start()
+    enter(section, me, ahead, behind)
+    offsets = []
+    for step in range(ups):
+        offsets.append(ups - step)
+        if step < downs:
+            offsets.append(step - downs)
+    offsets.append(0)
+    sides = {}
+    for slot, offset in enumerate(offsets):
+        block = ring_index(place + offset, count)
+        side = remote(
+            parts.at[1 - section, block],
+            theirs.at[block],
+            side_s.at[slot],
+            side_r.at[slot],
+            (1 - section, me),
+        )
+        side.start()
+        sides[offset] = side
+    keep.wait()
+
+    def local(offset):
+        sides[offset].wait_recv()
+        block = ring_index(place + offset, count)
+        return mine[block].astype(jnp.float32) + theirs[block].astype(jnp.float32)
+
+    ups_sent = []
+    downs_sent = []
+    for step in range(ups):
+        value = local(ups - step)
+        if step == 0:
+            held = first.at[0]
+        else:
+            ups_sent[-1].wait_recv()
+            held = up_buf.at[step - 1]
+            value = value + held[...].astype(jnp.float32)
+        held[...] = value.astype(held.dtype)
+        copy = remote(held, up_buf.at[step], up_s.at[step], up_r.at[step], (section, ahead))
+        copy.start()
+        ups_sent.append(copy)
+        if step < downs:
+            value = local(step - downs)
+            if step == 0:
+                held = first.at[1]
+            else:
+                downs_sent[-1].wait_recv()
+                held = down_buf.at[step - 1]
+                value = value + held[...].astype(jnp.float32)
+            held[...] = value.astype(held.dtype)
+            copy = remote(
+                held, down_buf.at[step], down_s.at[step], down_r.at[step], (section, behind)
+            )
+            copy.start()
+            downs_sent.append(copy)
+    value = local(0)
+    ups_sent[-1].wait_recv()
+    value = value + up_buf[ups - 1].astype(jnp.float32)
+    downs_sent[-1].wait_recv()
+    out[...] = value + down_buf[downs - 1].astype(jnp.float32)
+    for copy in ups_sent + downs_sent:
+        copy.wait_send()
+    for side in sides.values():
+        side.wait_send()
+
+
+def scatter_all(parts, count):
+    ups = count // 2
+    downs = count - 1 - ups
+    block = parts.shape[2:]
+    kind = parts.dtype
+    return pl.pallas_call(
+        lambda *refs: scatter_kernel(count, *refs),
+        out_shape=jax.ShapeDtypeStruct(block, jnp.float32),
+        in_specs=[pl.BlockSpec(memory_space=pl.ANY)],
+        out_specs=pl.BlockSpec(memory_space=pltpu.VMEM),
+        scratch_shapes=[
+            pltpu.VMEM((count,) + block, kind),
+            pltpu.VMEM((count,) + block, kind),
+            pltpu.VMEM((2,) + block, kind),
+            pltpu.VMEM((ups,) + block, kind),
+            pltpu.VMEM((downs,) + block, kind),
+            pltpu.SemaphoreType.DMA,
+            pltpu.SemaphoreType.DMA((ups,)),
+            pltpu.SemaphoreType.DMA((ups,)),
+            pltpu.SemaphoreType.DMA((ups,)),
+            pltpu.SemaphoreType.DMA((ups,)),
+            pltpu.SemaphoreType.DMA((count,)),
+            pltpu.SemaphoreType.DMA((count,)),
+        ],
+        compiler_params=pltpu.CompilerParams(collective_id=1, has_side_effects=True),
+        name="scatter_grads",
+    )(parts)
+
+
+EXTRA = 16
+
+
+def pack(qkv, proj, up, down, row):
+    owners = qkv.shape[0]
+    pieces = []
+    for matrix in (qkv, proj, up, down):
+        for start in range(0, matrix.shape[2], D):
+            pieces.append(matrix[:, :, start : start + D])
+    row = jnp.pad(row[:, None, :], ((0, 0), (0, EXTRA - 1), (0, D - row.shape[1])))
+    return jnp.concatenate(pieces + [row], 1).reshape(owners, -1, D)
+
+
+def unpack(packed, share, down_share, width):
+    start = 0
+    matrices = []
+    for extent, rows in ((3 * D, share), (D, share), (FF, share), (D, down_share)):
+        pieces = []
+        for _ in range(extent // D):
+            pieces.append(packed[:, start : start + rows])
+            start = start + rows
+        matrices.append(jnp.concatenate(pieces, 2).reshape(-1, extent))
+    return matrices, packed[:, start, :width].reshape(-1)
+
+
+def by_flag(flag, first, second):
+    return jnp.where(flag == 0, jnp.stack([first, second]), jnp.stack([second, first]))
+
+
+def swap_sections(value):
+    return lax.ppermute(value, "section", [(0, 1), (1, 0)])
+
+
+def whole_images(halves, section, half):
+    share = halves.shape[1] // (2 * lax.axis_size("section"))
+    own = lax.dynamic_slice_in_dim(halves, (section * 2 + half) * share, share, 1)
+    away = lax.dynamic_slice_in_dim(halves, (section * 2 + 1 - half) * share, share, 1)
+    both = by_flag(half, own, partner(away, "fsdp", 0))
+    both = both.transpose(1, 2, 3, 0, 4, 5, 6)
+    return both.reshape(both.shape[0], -1, SIDE, SIDE, D)
+
+
+def spread_images(first, second, section, half, groups):
+    mine = jnp.where(section == 0, first, second)
+    other = jnp.where(section == 0, second, first)
+    both = by_flag(section, mine, swap_sections(other))
+    both = both.reshape(both.shape[0], -1, groups, 2, WIN, SIDE, D)
+    kept = jnp.where(half == 0, both[:, :, :, 0], both[:, :, :, 1])
+    away = jnp.where(half == 0, both[:, :, :, 1], both[:, :, :, 0])
+    halves = by_flag(half, kept, partner(away, "fsdp", 0))
+    return halves.transpose(1, 0, 2, 3, 4, 5, 6).reshape(-1, groups, WIN, SIDE, D)
 
 
 def on_device(
     block_input, cotangent, qkv_weight, proj_weight, fc1_weight, fc2_weight, vectors, rel_table
 ):
     section = lax.axis_index("section")
-    shifted = section == 1
+    sections = lax.axis_size("section")
+    half = lax.axis_index("fsdp") % 2
+    count = lax.axis_size("fsdp")
+    groups = block_input.shape[1]
+    share = qkv_weight.shape[1]
+    down_share = fc2_weight.shape[1]
+    width = vectors.shape[1]
     onehot = relative_onehot()
-    allowed = allowed_pairs(lax.axis_index("fsdp") % 2 * WIN, WIN, shifted)
-    shards = (qkv_weight[0], proj_weight[0], fc1_weight[0], fc2_weight[0], vectors[0])
-    gathered = (
-        lax.all_gather(shards[0], "fsdp", axis=0, tiled=True),
-        lax.all_gather(shards[1], "fsdp", axis=0, tiled=True),
-        lax.all_gather(shards[2], "fsdp", axis=0, tiled=True),
-        lax.all_gather(shards[3], "fsdp", axis=0, tiled=True),
-        lax.all_gather(shards[4], "fsdp", axis=0, tiled=True),
-    )
-    weights = gathered[:4]
-    vector_row = gathered[4]
-    table = rel_table[0]
-    count = block_input.shape[0]
-    kept = jnp.zeros(block_input.shape, jnp.bfloat16)
-    produced = jnp.zeros(block_input.shape, jnp.bfloat16)
-    incoming = jnp.zeros(block_input.shape[1:], jnp.bfloat16)
-    for tick in range(count + 1):
-        micro = tick - section
-        valid = (micro >= 0) & (micro < count)
-        place = jnp.clip(micro, 0, count - 1)
-        source = jnp.where(section == 0, block_input[min(tick, count - 1)], incoming)
-        rolled = jnp.where(shifted, roll_rows_in(source, strip_swap), source)
-        result = block_forward(rolled, weights, vector_row, table, allowed, onehot).astype(
-            jnp.bfloat16
-        )
-        output = jnp.where(shifted, roll_rows_out(result, strip_swap), result)
-        kept = jnp.where(valid, kept.at[place].set(rolled), kept)
-        produced = jnp.where(valid, produced.at[place].set(output), produced)
-        if tick < count:
-            incoming = from_behind(output, "section", 1)
-    sums = tuple((jnp.zeros(piece.shape, jnp.float32) for piece in gathered))
-    table_sum = jnp.zeros(table.shape, jnp.float32)
-    returned = jnp.zeros(block_input.shape, jnp.float32)
-    incoming_grad = jnp.zeros(block_input.shape[1:], jnp.float32)
-    for tick in range(count + 1):
-        micro = tick - 1 + section
-        valid = (micro >= 0) & (micro < count)
-        place = jnp.clip(micro, 0, count - 1)
-        arriving = jnp.where(
-            section == 1, cotangent[min(tick, count - 1)].astype(jnp.float32), incoming_grad
-        )
-        grad_in = jnp.where(shifted, roll_rows_in(arriving, grad_swap), arriving)
-        grad_grid, grads, grad_table = block_backward(
-            kept[place], grad_in, weights, vector_row, table, allowed, onehot
-        )
-        grad_source = jnp.where(shifted, roll_rows_out(grad_grid, grad_swap), grad_grid)
-        sums = tuple((jnp.where(valid, total + part, total) for total, part in zip(sums, grads)))
-        table_sum = jnp.where(valid, table_sum + grad_table, table_sum)
-        returned = jnp.where(valid, returned.at[place].set(grad_source), returned)
-        if tick < count:
-            incoming_grad = from_behind(grad_source.astype(jnp.bfloat16), "section", -1).astype(
-                grad_source.dtype
-            )
-    scattered = (
-        lax.psum_scatter(sums[0], "fsdp", scatter_dimension=0, tiled=True),
-        lax.psum_scatter(sums[1], "fsdp", scatter_dimension=0, tiled=True),
-        lax.psum_scatter(sums[2], "fsdp", scatter_dimension=0, tiled=True),
-        lax.psum_scatter(sums[3], "fsdp", scatter_dimension=0, tiled=True),
-        lax.psum_scatter(sums[4], "fsdp", scatter_dimension=0, tiled=True),
-    )
-    table_total = lax.psum(table_sum, "fsdp")
+    gathered = gather_all(
+        pack(qkv_weight, proj_weight, fc1_weight, fc2_weight, vectors)[0], sections, count
+    )
+    images = whole_images(jnp.stack([block_input, cotangent]), section, half)
+    tables = by_flag(section, rel_table[0], swap_sections(rel_table[0]))
+    layers = [unpack(gathered[layer], share, down_share, width) for layer in range(2)]
+    masks = (None, allowed_pairs())
+
+    def forward(grid, layer):
+        weights, row = layers[layer]
+        result, saved = recompute(grid, weights, row, tables[layer], masks[layer], onehot)
+        batch = grid.shape[0]
+        out = from_windows(result.reshape(-1, WIN * WIN, D).astype(jnp.bfloat16), batch, SIDE, SIDE)
+        return out, saved
+
+    first_out, first_saved = forward(images[0], 0)
+    second_out, second_saved = forward(jnp.roll(first_out, (-SHIFT, -SHIFT), (1, 2)), 1)
+    second_out = jnp.roll(second_out, (SHIFT, SHIFT), (1, 2))
+    grad = jnp.roll(images[1], (-SHIFT, -SHIFT), (1, 2)).astype(jnp.float32)
+    second_grid, second_grads, second_table = block_backward(
+        second_saved, grad, layers[1][0], onehot
+    )
+    second_grid = jnp.roll(second_grid, (SHIFT, SHIFT), (1, 2))
+    first_grid, first_grads, first_table = block_backward(
+        first_saved, second_grid, layers[0][0], onehot
+    )
+
+    def owners(grads):
+        shaped = [piece.reshape(count, -1, piece.shape[-1]) for piece in grads[:4]]
+        return pack(*shaped, grads[4].reshape(count, -1)).astype(jnp.bfloat16)
+
+    summed = scatter_all(jnp.stack([owners(first_grads), owners(second_grads)]), count)
+    mine, row = unpack(summed[None], share, down_share, width)
+    table_total = lax.psum(jnp.stack([first_table, second_table]), ("section", "fsdp"))
+    table_total = jnp.where(section == 0, table_total[0], table_total[1])
+    produced = spread_images(first_out, second_out, section, half, groups)
+    returned = spread_images(
+        first_grid.astype(jnp.bfloat16), second_grid.astype(jnp.bfloat16), section, half, groups
+    ).astype(jnp.float32)
     return (
         produced[None],
         returned[None],
-        scattered[0][None],
-        scattered[1][None],
-        scattered[2][None],
-        scattered[3][None],
-        scattered[4][None],
+        mine[0][None],
+        mine[1][None],
+        mine[2][None],
+        mine[3][None],
+        row[None],
         table_total[None],
     )
 

time: 1170 us -> 597 us (0.51)
  waiting for transfers between devices: 287 us -> 0.02 us
  Pallas kernels: 0 us -> 171 us
  matrix products: 229 us -> 84.4 us
  local copies, waits for them, and re-layouts: 354 us -> 218 us
  blocking collectives: 156 us -> 38.9 us
  starting transfers between devices: 39.2 us -> 5.61 us
  between operations: 20 us -> 3.1 us
    reduce_scatter x4 -> x0, waiting for transfers between devices: 173 us -> none  [the longest x1 97.7 us: on_device(): lax.psum_scatter(sums[3], 'fsdp', scatter_dimension=0, tiled=True)]
    pallas_call x0 -> x2, Pallas kernels: none -> 171 us  [the longest x1 88.4 us: gather_all(): pl.pallas_call(lambda *refs: gather_kernel(count, *refs), out_shape=jax.S...]
    all_gather x3 -> x0, waiting for transfers between devices: 90.7 us -> none  [the longest x1 62 us: on_device(): lax.all_gather(shards[2], 'fsdp', axis=0, tiled=True)]
    all_gather x2 -> x0, blocking collectives: 80 us -> none  [the longest x1 40.4 us: on_device(): lax.all_gather(shards[4], 'fsdp', axis=0, tiled=True)]
    unnamed x1 -> x0, blocking collectives: 76.5 us -> none
    dot_general x40 -> x10, matrix products: 77.6 us -> 19.4 us  [batched(): return jnp.einsum(form, first, second, preferred_element_type=jnp.float32)]
    unnamed x688 -> x353, local copies, waits for them, and re-layouts: 77.3 us -> 30.7 us
    psum x0 -> x1, blocking collectives: none -> 38.9 us  [on_device(): lax.psum(jnp.stack([first_table, second_table]), ('section', 'fsdp'))]
  transfers between devices with their start and end apart: 35 -> 6, of which waited for: 22 -> 0; matrix products, arithmetic and copies ran while one was open for 25% -> 17% of each run, Pallas kernels for 0% -> 29%
where the time goes in v1:
time: 597 us; the launch traced here: 590 us
  local copies, waits for them, and re-layouts  218 us (37%)
  Pallas kernels  171 us (29%)
  matrix products  84.4 us (14%)
  other arithmetic  67.8 us (11%)
  blocking collectives  38.9 us (7%)
    pallas_call x1, Pallas kernels, gather_all(): pl.pallas_call(lambda *refs: gather_kernel(count, *refs), out_shape=jax.S...  88.4 us
    pallas_call x1, Pallas kernels, scatter_all(): pl.pallas_call(lambda *refs: scatter_kernel(count, *refs), out_shape=jax....  82.9 us
    psum x1, blocking collectives, on_device(): lax.psum(jnp.stack([first_table, second_table]), ('section', 'fsdp'))  38.9 us
    unnamed x353, local copies, waits for them, and re-layouts  30.7 us
    dot_general x8, matrix products, plain_product(): return jnp.dot(first, second, preferred_element_type=jnp.float32)  20.7 us
    dot_general x10, matrix products, batched(): return jnp.einsum(form, first, second, preferred_element_type=jnp.float32)  19.4 us
    dot_general x8, matrix products, right_product(): lax.dot_general(first, second, (((1,), (1,)), ((), ())), preferred_elemen...  18.2 us
    slice x5, local copies, waits for them, and re-layouts, unpack(): pieces.append(packed[:, start:start + rows])  13.2 us
  transfers between devices with their start and end apart: 6, of which 0 were waited for; matrix products, arithmetic and copies ran while one was open for 17% of the time, Pallas kernels for 29%

profile of v1, /device:TPU:0, one launch (start us, length us, event | category | flops | bytes accessed | tf_op | source)
XLA Modules:
  0.0 589.5 jit_solution(7819990277105616598)
XLA Ops:
  1.2 3.2 fusion.126
  7.9 88.4 %gather_weights.1 = bf16[2,16,400,512]{3,2,1,0:T(8,128)(2,1)} custom-call(bf16[400,512]{1,0:T(8,128)(2,1)} %bitcast.505), custom_call_target="tpu_custom_call" | custom-call | tf_op jit(solution)/shard_map/gather_weights/pallas_call | solution.py:309
  96.3 5.9 slice_bitcast_fusion
  103.0 3.5 fusion.165
  119.9 3.1 slice.495
  123.0 3.2 slice.468
  129.6 3.5 fusion.3
  135.1 3.5 fusion.5
  172.6 3.0 copy.855
  179.6 3.4 fusion.175
  190.9 5.4 fusion.10
  219.3 5.7 fusion.14
  253.8 2.6 copy.874
  256.4 4.2 fusion.177
  267.8 6.6 %fusion.17 = (bf16[2048,196]{0,1:T(8,128)(2,1)}, f32[196,2048]{1,0:T(8,128)S(1)}) fusion(f32[2048]{0:T(1024)S(1)} %copy-done.136, bf16[512,2048]{1,0:T(8,128)(2,1)} %bitcast.478, f32[196,512]{1,0:T(8,128)S(1)} %get-tuple-element.126, f32[512]{0:T(512)S(1)} %copy-done.140, f32[512]{0:T(512)S(1)} %copy-done.101, f32[196]{0:T(256)S(1)} %fusion.146, ...), kind=kOutput, calls=%fused_computation.42 | convolution fusion | flops 438036480 | bytes 4920864 | tf_op jit(solution)/shard_map/dot_general | solution.py:26
  274.5 6.1 %fusion.159 = (bf16[2048]{0:T(1024)(128)(2,1)}, bf16[196,2048]{1,0:T(8,128)(2,1)}, f32[196,2048]{1,0:T(8,128)S(1)}) fusion(f32[196,2048]{1,0:T(8,128)S(1)} %get-tuple-element.138, bf16[196,512]{1,0:T(8,128)(2,1)S(1)} %copy-done.28, bf16[2048,512]{1,0:T(8,128)(2,1)S(1)} %bitcast.454), kind=kOutput, calls=%fused_computation.370 | convolution fusion | flops 440342528 | bytes 6316032 | tf_op jit(solution)/shard_map/dot_general | solution.py:36
  296.0 3.5 multiply_reduce_fusion.2
  303.9 2.6 copy.896
  306.5 3.7 fusion.169
  349.6 4.5 fusion.155
  360.9 3.8 fusion.167
  412.0 38.9 %psum.7 = f32[2,169,16]{1,2,0:T(8,128)S(1)} all-reduce(f32[2,169,16]{1,2,0:T(8,128)} %pad_maximum_fusion.15), channel_id=1, replica_groups=mesh['section'=2,'fsdp'=16] {'section','fsdp'}, use_global_device_ids=true, to_apply=%region_43.44 | all-reduce | flops 5408 | bytes 43264 | tf_op jit(solution)/shard_map/psum | solution.py:546
  476.8 5.6 pad_maximum_fusion.refs_0_
  482.4 82.9 %scatter_grads.1 = f32[400,512]{1,0:T(8,128)} custom-call(bf16[2,16,400,512]{3,2,1,0:T(8,128)(2,1)} %pad_maximum_fusion.refs_0_), custom_call_target="tpu_custom_call" | custom-call | tf_op jit(solution)/shard_map/scatter_grads/pallas_call | solution.py:424
  (620 shorter events, 289.6 us)
Async XLA Ops:
  0.7 127.5 %collective-permute-start.1 = (f32[169,16]{0,1:T(8,128)}, f32[169,16]{0,1:T(8,128)}, u32[]{:S(2)}, u32[]{:S(2)}) collective-permute-start(f32[169,16]{0,1:T(8,128)} %bitcast.516), channel_id=1, source_target_pairs={{0,16},{16,0},{1,17},{17,1},{2,18},{18,2},{3,19},{19,3},{4,20},{20... | collective-permute-start | bytes 32456 | tf_op jit(solution)/shard_map/ppermute | solution.py:478
  4.4 136.2 %collective-permute-start = (bf16[2,1,1,7,14,512]{5,1,4,3,2,0:T(2,128)(2,1)}, bf16[2,1,1,7,14,512]{5,1,4,3,2,0:T(2,128)(2,1)}, u32[]{:S(2)}, u32[]{:S(2)}) collective-permute-start(bf16[2,1,1,7,14,512]{5,1,4,3,2,0:T(2,128)(2,1)} %get-tuple-element.86), channel_id=1, source_target_pairs={{0,1},{1,0},{2,3},{3,2},{4,5},{5,4},{6,7},{7,6},{8,9},{9,8},{10,11... | collective-permute-start | bytes 602120 | tf_op jit(solution)/shard_map/ppermute | solution.py:22
  103.0 6.9 %copy-start.88 = (f32[16,1,384]{2,1,0:T(1,128)}, f32[16,1,384]{2,1,0:T(1,128)S(1)}, u32[]{:S(2)}) copy-start(f32[16,1,384]{2,1,0:T(1,128)S(1)} %get-tuple-element.142) | copy-start | bytes 73732
  110.5 52.5 %copy-start.91 = (f32[512]{0:T(512)}, f32[512]{0:T(512)S(1)}, u32[]{:S(2)}) copy-start(f32[512]{0:T(512)S(1)} %get-tuple-element.116) | copy-start | bytes 6148
  110.5 52.5 %copy-start.96 = (f32[512]{0:T(512)}, f32[512]{0:T(512)S(1)}, u32[]{:S(2)}) copy-start(f32[512]{0:T(512)S(1)} %get-tuple-element.115) | copy-start | bytes 6148
  152.0 7.6 %copy-start.74 = (f32[2,2,7,7]{0,3,1,2:T(8,128)S(1)}, f32[2,2,7,7]{0,3,1,2:T(8,128)}, u32[]{:S(2)}) copy-start(f32[2,2,7,7]{0,3,1,2:T(8,128)} %multiply_reduce_fusion.13) | copy-start | bytes 2356
  156.1 6.9 %copy-start.55 = (f32[2,2,7,7]{0,3,1,2:T(8,128)S(1)}, f32[2,2,7,7]{0,3,1,2:T(8,128)}, u32[]{:S(2)}) copy-start(f32[2,2,7,7]{0,3,1,2:T(8,128)} %broadcast_multiply_fusion.1) | copy-start | bytes 2356
  190.9 7.2 %copy-start.8 = (bf16[16,128,512]{2,1,0:T(8,128)(2,1)S(1)}, bf16[16,128,512]{2,1,0:T(8,128)(2,1)}, u32[]{:S(2)}) copy-start(bf16[16,128,512]{2,1,0:T(8,128)(2,1)} %slice.468) | copy-start | bytes 6291460
  190.9 7.2 %copy-start.131 = (f32[512]{0:T(512)S(1)}, f32[512]{0:T(512)}, u32[]{:S(2)}) copy-start(f32[512]{0:T(512)} %get-tuple-element.109) | copy-start | bytes 6148
  267.5 13.1 %copy-start.2 = (f32[196,512]{1,0:T(8,128)}, f32[196,512]{1,0:T(8,128)S(1)}, u32[]{:S(2)}) copy-start(f32[196,512]{1,0:T(8,128)S(1)} %get-tuple-element.126) | copy-start | bytes 1204228
  267.6 6.9 %copy-start.109 = (f32[196]{0:T(256)}, f32[196]{0:T(256)S(1)}, u32[]{:S(2)}) copy-start(f32[196]{0:T(256)S(1)} %broadcast_multiply_fusion.3) | copy-start | bytes 2356
  397.5 7.4 %copy-start.23 = (bf16[196,1536]{1,0:T(8,128)(2,1)S(1)}, bf16[196,1536]{1,0:T(8,128)(2,1)}, u32[]{:S(2)}) copy-start(bf16[196,1536]{1,0:T(8,128)(2,1)} %copy-done.22) | copy-start | bytes 1806340
  398.3 171.6 %collective-permute-start.2 = (bf16[1,14,14,512]{3,1,2,0:T(8,128)(2,1)}, bf16[1,14,14,512]{3,1,2,0:T(8,128)(2,1)}, u32[]{:S(2)}, u32[]{:S(2)}) collective-permute-start(bf16[1,14,14,512]{3,1,2,0:T(8,128)(2,1)} %maximum_select_fusion), channel_id=1, source_target_pairs={{0,16},{16,0},{1,17},{17,1},{2,18},{18,2},{3,19},{19,3},{4,20},{20... | collective-permute-start | bytes 602120 | tf_op jit(solution)/shard_map/ppermute | solution.py:478
  405.4 45.5 %copy-start.113 = (bf16[16,32]{1,0:T(8,128)(2,1)S(1)}, bf16[16,32]{1,0:T(8,128)(2,1)}, u32[]{:S(2)}) copy-start(bf16[16,32]{1,0:T(8,128)(2,1)} %get-tuple-element.71) | copy-start | bytes 3076
  405.5 46.1 %copy-start.134 = (f32[512]{0:T(512)S(1)}, f32[512]{0:T(512)}, u32[]{:S(2)}) copy-start(f32[512]{0:T(512)} %get-tuple-element.22) | copy-start | bytes 6148
  405.5 46.1 %copy-start.135 = (f32[512]{0:T(512)S(1)}, f32[512]{0:T(512)}, u32[]{:S(2)}) copy-start(f32[512]{0:T(512)} %get-tuple-element.20) | copy-start | bytes 6148
  405.5 62.0 %copy-start.17 = (f32[1,14,11,512]{3,1,2,0:T(8,128)S(1)}, f32[1,14,11,512]{3,1,2,0:T(8,128)}, u32[]{:S(2)}) copy-start(f32[1,14,11,512]{3,1,2,0:T(8,128)} %copy-done.16) | copy-start | bytes 946180
  405.5 61.9 %copy-start.54 = (f32[1,14,3,512]{3,1,2,0:T(8,128)S(1)}, f32[1,14,3,512]{3,1,2,0:T(8,128)}, u32[]{:S(2)}) copy-start(f32[1,14,3,512]{3,1,2,0:T(8,128)} %copy-done.53) | copy-start | bytes 258052
  407.7 61.6 %copy-start.25 = (bf16[196,1536]{1,0:T(8,128)(2,1)S(1)}, bf16[196,1536]{1,0:T(8,128)(2,1)}, u32[]{:S(2)}) copy-start(bf16[196,1536]{1,0:T(8,128)(2,1)} %copy-done.24) | copy-start | bytes 1806340
  468.2 104.8 %collective-permute-start.4 = (bf16[1,14,14,512]{3,1,2,0:T(8,128)(2,1)}, bf16[1,14,14,512]{3,1,2,0:T(8,128)(2,1)}, u32[]{:S(2)}, u32[]{:S(2)}) collective-permute-start(bf16[1,14,14,512]{3,1,2,0:T(8,128)(2,1)} %convert_select_fusion), channel_id=1, source_target_pairs={{0,16},{16,0},{1,17},{17,1},{2,18},{18,2},{3,19},{19,3},{4,20},{20... | collective-permute-start | bytes 602120 | tf_op jit(solution)/shard_map/ppermute | solution.py:478
  482.4 84.7 %copy-start.63 = (bf16[1,2,7,2,7,512]{5,1,4,3,2,0:T(2,128)(2,1)S(1)}, bf16[1,2,7,2,7,512]{5,1,4,3,2,0:T(2,128)(2,1)}, u32[]{:S(2)}) copy-start(bf16[1,2,7,2,7,512]{5,1,4,3,2,0:T(2,128)(2,1)} %copy.860) | copy-start | bytes 602116
  482.4 84.7 %copy-start.67 = (bf16[1,2,7,11,512]{4,1,3,2,0:T(2,128)(2,1)S(1)}, bf16[1,2,7,11,512]{4,1,3,2,0:T(2,128)(2,1)}, u32[]{:S(2)}) copy-start(bf16[1,2,7,11,512]{4,1,3,2,0:T(2,128)(2,1)} %copy.881) | copy-start | bytes 473092
  572.9 9.2 %collective-permute-start.3 = (bf16[2,1,1,7,14,512]{5,0,4,3,2,1:T(2,128)(2,1)S(1)}, bf16[2,1,1,7,14,512]{5,0,4,3,2,1:T(2,128)(2,1)S(1)}, u32[]{:S(2)}, u32[]{:S(2)}) collective-permute-start(bf16[2,1,1,7,14,512]{5,0,4,3,2,1:T(2,128)(2,1)S(1)} %bitcast.508), channel_id=1, source_target_pairs={{0,1},{1,0},{2,3},{3,2},{4,5},{5,4},{6,7},{7,6},{8,9},{9,8},{10,11... | collective-permute-start | bytes 602120 | tf_op jit(solution)/shard_map/ppermute | solution.py:22
  576.0 9.6 %collective-permute-start.5 = (bf16[2,1,1,7,14,512]{5,0,4,3,2,1:T(2,128)(2,1)S(1)}, bf16[2,1,1,7,14,512]{5,0,4,3,2,1:T(2,128)(2,1)S(1)}, u32[]{:S(2)}, u32[]{:S(2)}) collective-permute-start(bf16[2,1,1,7,14,512]{5,0,4,3,2,1:T(2,128)(2,1)S(1)} %bitcast.510), channel_id=1, source_target_pairs={{0,1},{1,0},{2,3},{3,2},{4,5},{5,4},{6,7},{7,6},{8,9},{9,8},{10,11... | collective-permute-start | bytes 602120 | tf_op jit(solution)/shard_map/ppermute | solution.py:22
  (135 other events, 398.4 us)

commit v2 on v1

--- a/solution.py
+++ b/solution.py
@@ -36,17 +36,6 @@
     return lax.dot_general(
         first, second, (((1,), (1,)), ((), ())), preferred_element_type=jnp.float32
     )
-
-
-def batched(form, first, second):
-    return jnp.einsum(form, first, second, preferred_element_type=jnp.float32)
-
-
-def layer_norm(values, gain, offset):
-    average = jnp.mean(values, -1, keepdims=True)
-    centred = values - average
-    spread = jnp.mean(centred * centred, -1, keepdims=True)
-    return centred * lax.rsqrt(spread + EPS) * gain + offset
 
 
 def to_windows(grid):
@@ -88,117 +77,267 @@
     )
 
 
-def split_vectors(vector_row):
-    values = vector_row.astype(jnp.float32)
-    pieces = []
-    start = 0
-    for extent in [D] * 7 + [FF, D]:
-        pieces.append(values[start : start + extent])
-        start = start + extent
-    return pieces
-
-
-def recompute(grid_b, weights, vector_row, table, allowed, onehot):
-    w_qkv, w_proj, w_up, w_down = weights
-    parts = split_vectors(vector_row)
-    base = to_windows(grid_b.astype(jnp.float32)).reshape(-1, D)
-    normed = layer_norm(base, parts[0], parts[1]).astype(jnp.bfloat16)
-    table_bias = jnp.dot(onehot, table, precision=lax.Precision.HIGHEST)
-    table_bias = table_bias.reshape(WIN * WIN, WIN * WIN, H).transpose(2, 0, 1)
-    mixed = plain_product(normed, w_qkv)
-    scale = HD ** (-0.5)
-    query = ((mixed[:, :D] + parts[2]) * scale).astype(jnp.bfloat16).reshape(-1, WIN * WIN, H, HD)
-    keys = mixed[:, D : 2 * D].astype(jnp.bfloat16).reshape(-1, WIN * WIN, H, HD)
-    values = (mixed[:, 2 * D :] + parts[3]).astype(jnp.bfloat16).reshape(-1, WIN * WIN, H, HD)
-    scores = batched("wihd,wjhd->whij", query, keys) + table_bias[None]
+PADDED = 64
+LANES = 128
+BLOCKS = 12
+FAR = -1e30
+
+
+def normalise(values):
+    centred = values - jnp.mean(values, -1, keepdims=True)
+    inverse = lax.rsqrt(jnp.mean(centred * centred, -1, keepdims=True) + EPS)
+    return centred * inverse, inverse
+
+
+def normalise_back(scaled, inverse, gain, grad):
+    inner = grad * gain
+    first = jnp.mean(inner, -1, keepdims=True)
+    second = jnp.mean(inner * scaled, -1, keepdims=True)
+    return inverse * (inner - first - scaled * second)
+
+
+def block_of(ref, index):
+    owners, rows, _ = ref.shape
+    share = D // owners
+    if index < 8:
+        return (slice(None), slice(index * share, (index + 1) * share))
+    part = index - 8
+    if owners == 1:
+        return (slice(None), slice(index * D, (index + 1) * D))
+    quarter = owners // 4
+    return (slice(part * quarter, (part + 1) * quarter), slice(8 * share, 12 * share))
+
+
+def weight(ref, index):
+    return ref[block_of(ref, index)].reshape(D, D)
+
+
+def put(ref, index, value):
+    place = block_of(ref, index)
+    shape = ref[place].shape
+    ref[place] = value.astype(ref.dtype).reshape(shape)
+
+
+def head_lanes(head):
+    lane = lax.broadcasted_iota(jnp.int32, (1, LANES), 1)
+    return lane // HD == head
+
+
+def spread_heads(piece):
+    zero = jnp.zeros_like(piece)
+    return jnp.concatenate([jnp.where(head_lanes(h), piece, zero) for h in range(LANES // HD)], 0)
+
+
+def join_heads(tall):
+    rows = tall.shape[0] // (LANES // HD)
+    total = jnp.where(head_lanes(0), tall[:rows], 0.0)
+    for h in range(1, LANES // HD):
+        total = total + jnp.where(head_lanes(h), tall[h * rows : (h + 1) * rows], 0.0)
+    return total
+
+
+def cols(index, width=D):
+    return slice(index * width, (index + 1) * width)
+
+
+def forward_kernel(x, w, vec, bias, out, normed, mixed, soft, att, mid, second, up, act):
+    base = x[...].astype(jnp.float32)
+    scaled, _ = normalise(base)
+    normed[...] = (scaled * vec[0:1] + vec[1:2]).astype(jnp.bfloat16)
+    query = plain_product(normed[...], weight(w, 0))
+    mixed[:, cols(0)] = ((query + vec[2:3]) * HD ** (-0.5)).astype(jnp.bfloat16)
+    mixed[:, cols(1)] = plain_product(normed[...], weight(w, 1)).astype(jnp.bfloat16)
+    values = plain_product(normed[...], weight(w, 2))
+    mixed[:, cols(2)] = (values + vec[3:4]).astype(jnp.bfloat16)
+    groups = D // LANES
+    for window in range(x.shape[0] // PADDED):
+        rows = cols(window, PADDED)
+        for group in range(groups):
+            q = spread_heads(mixed[rows, cols(group, LANES)])
+            k = mixed[rows, cols(groups + group, LANES)]
+            v = mixed[rows, cols(2 * groups + group, LANES)]
+            scores = right_product(q, k) + bias[window % bias.shape[0], group]
+            expo = jnp.exp(scores - jnp.max(scores, -1, keepdims=True))
+            prob = expo / jnp.sum(expo, -1, keepdims=True)
+            soft[window * groups + group] = prob
+            tall = plain_product(prob.astype(jnp.bfloat16), v)
+            att[rows, cols(group, LANES)] = join_heads(tall).astype(jnp.bfloat16)
+    middle = base + plain_product(att[...], weight(w, 3)) + vec[4:5]
+    mid[...] = middle
+    scaled, _ = normalise(middle)
+    second[...] = (scaled * vec[5:6] + vec[6:7]).astype(jnp.bfloat16)
+    total = middle + vec[11:12]
+    for part in range(FF // D):
+        upward = plain_product(second[...], weight(w, 4 + part)) + vec[7 + part : 8 + part]
+        up[:, cols(part)] = upward
+        activated = (0.5 * upward * (1.0 + lax.erf(upward * 0.5**0.5))).astype(jnp.bfloat16)
+        act[:, cols(part)] = activated
+        total = total + plain_product(activated, weight(w, 8 + part))
+    out[...] = total.astype(jnp.bfloat16)
+
+
+def backward_kernel(
+    grad, x, w, vec, normed, mixed, soft, att, mid, second, up, act, dx, dw, dvec, dscore, datt, dmix
+):
+    grad_out = grad[...]
+    down_in = grad_out.astype(jnp.bfloat16)
+    grad_second = jnp.zeros(grad_out.shape, jnp.float32)
+    for part in range(FF // D):
+        grad_act = right_product(down_in, weight(w, 8 + part))
+        upward = up[:, cols(part)]
+        slope = 0.5 * (1.0 + lax.erf(upward * 0.5**0.5))
+        slope = slope + upward * jnp.exp(-0.5 * upward * upward) * 0.3989422804014327
+        grad_up = grad_act * slope
+        dvec[7 + part : 8 + part] = jnp.sum(grad_up, 0, keepdims=True)
+        up_in = grad_up.astype(jnp.bfloat16)
+        put(dw, 4 + part, left_product(second[...], up_in))
+        put(dw, 8 + part, left_product(act[:, cols(part)], down_in))
+        grad_second = grad_second + right_product(up_in, weight(w, 4 + part))
+    dvec[11:12] = jnp.sum(grad_out, 0, keepdims=True)
+    scaled, inverse = normalise(mid[...])
+    dvec[5:6] = jnp.sum(grad_second * scaled, 0, keepdims=True)
+    dvec[6:7] = jnp.sum(grad_second, 0, keepdims=True)
+    grad_mid = grad_out + normalise_back(scaled, inverse, vec[5:6], grad_second)
+    dvec[4:5] = jnp.sum(grad_mid, 0, keepdims=True)
+    proj_in = grad_mid.astype(jnp.bfloat16)
+    put(dw, 3, left_product(att[...], proj_in))
+    datt[...] = right_product(proj_in, weight(w, 3)).astype(jnp.bfloat16)
+    groups = D // LANES
+    for group in range(groups):
+        lanes = cols(group, LANES)
+        scores_sum = jnp.zeros(dscore.shape[1:], jnp.float32)
+        query_sum = jnp.zeros((1, LANES), jnp.float32)
+        value_sum = jnp.zeros((1, LANES), jnp.float32)
+        for window in range(x.shape[0] // PADDED):
+            rows = cols(window, PADDED)
+            q = spread_heads(mixed[rows, lanes])
+            k = mixed[rows, cols(groups + group, LANES)]
+            v = mixed[rows, cols(2 * groups + group, LANES)]
+            prob = soft[window * groups + group]
+            away = spread_heads(datt[rows, lanes])
+            grad_soft = right_product(away, v)
+            grad_values = left_product(prob.astype(jnp.bfloat16), away)
+            total = jnp.sum(prob * grad_soft, -1, keepdims=True)
+            grad_scores = prob * (grad_soft - total)
+            scores_sum = scores_sum + grad_scores
+            scores_b = grad_scores.astype(jnp.bfloat16)
+            grad_query = join_heads(plain_product(scores_b, k)) * HD ** (-0.5)
+            grad_keys = left_product(scores_b, q)
+            query_sum = query_sum + jnp.sum(grad_query, 0, keepdims=True)
+            value_sum = value_sum + jnp.sum(grad_values, 0, keepdims=True)
+            dmix[rows, lanes] = grad_query.astype(jnp.bfloat16)
+            dmix[rows, cols(groups + group, LANES)] = grad_keys.astype(jnp.bfloat16)
+            dmix[rows, cols(2 * groups + group, LANES)] = grad_values.astype(jnp.bfloat16)
+        dscore[group] = scores_sum
+        dvec[2:3, lanes] = query_sum
+        dvec[3:4, lanes] = value_sum
+    grad_normed = jnp.zeros(grad_out.shape, jnp.float32)
+    for part in range(3):
+        piece = dmix[:, cols(part)]
+        put(dw, part, left_product(normed[...], piece))
+        grad_normed = grad_normed + right_product(piece, weight(w, part))
+    scaled, inverse = normalise(x[...].astype(jnp.float32))
+    dvec[0:1] = jnp.sum(grad_normed * scaled, 0, keepdims=True)
+    dvec[1:2] = jnp.sum(grad_normed, 0, keepdims=True)
+    dx[...] = grad_mid + normalise_back(scaled, inverse, vec[0:1], grad_normed)
+
+
+def in_vmem(count):
+    return [pl.BlockSpec(memory_space=pltpu.VMEM)] * count
+
+
+def shaped(kind, *shape):
+    return jax.ShapeDtypeStruct(shape, kind)
+
+
+def run_forward(x, w, vec, bias):
+    rows = x.shape[0]
+    half, full = jnp.bfloat16, jnp.float32
+    units = rows // PADDED * (D // LANES)
+    shapes = (
+        shaped(half, rows, D),
+        shaped(half, rows, D),
+        shaped(half, rows, 3 * D),
+        shaped(full, units, PADDED * LANES // HD, PADDED),
+        shaped(half, rows, D),
+        shaped(full, rows, D),
+        shaped(half, rows, D),
+        shaped(full, rows, FF),
+        shaped(half, rows, FF),
+    )
+    return pl.pallas_call(
+        forward_kernel,
+        out_shape=shapes,
+        in_specs=in_vmem(4),
+        out_specs=tuple(in_vmem(len(shapes))),
+        compiler_params=pltpu.CompilerParams(vmem_limit_bytes=56 << 20),
+        name="layer_forward",
+    )(x, w, vec, bias)
+
+
+def run_backward(grad, x, w, vec, saved):
+    rows = x.shape[0]
+    half, full = jnp.bfloat16, jnp.float32
+    shapes = (
+        shaped(full, rows, D),
+        shaped(half, w.shape[0], BLOCKS * D // w.shape[0], D),
+        shaped(full, BLOCKS, D),
+        shaped(full, D // LANES, PADDED * LANES // HD, PADDED),
+    )
+    return pl.pallas_call(
+        backward_kernel,
+        out_shape=shapes,
+        in_specs=in_vmem(4 + len(saved)),
+        out_specs=tuple(in_vmem(len(shapes))),
+        scratch_shapes=[pltpu.VMEM((rows, D), half), pltpu.VMEM((rows, 3 * D), half)],
+        compiler_params=pltpu.CompilerParams(vmem_limit_bytes=56 << 20),
+        name="layer_backward",
+    )(grad, x, w, vec, *saved)
+
+
+def pad_windows(grid):
+    tokens = to_windows(grid)
+    return jnp.pad(tokens, ((0, 0), (0, PADDED - WIN * WIN), (0, 0))).reshape(-1, D)
+
+
+def unpad_windows(rows, batch):
+    return from_windows(rows.reshape(-1, PADDED, D)[:, : WIN * WIN], batch, SIDE, SIDE)
+
+
+def score_bias(table, allowed, onehot):
+    bias = jnp.dot(onehot, table, precision=lax.Precision.HIGHEST)
+    bias = bias.reshape(WIN * WIN, WIN * WIN, H).transpose(2, 0, 1)[None]
     if allowed is not None:
-        windows = allowed.shape[0]
-        scores = scores.reshape((-1, windows) + scores.shape[1:])
-        scores = jnp.where(allowed[None, :, None], scores, -jnp.inf)
-        scores = scores.reshape((-1,) + scores.shape[2:])
-    highest = jnp.max(scores, -1, keepdims=True)
-    expo = jnp.exp(scores - highest)
-    soft = expo / jnp.sum(expo, -1, keepdims=True)
-    attended = (
-        batched("whij,wjhd->wihd", soft.astype(jnp.bfloat16), values)
-        .astype(jnp.bfloat16)
-        .reshape(-1, D)
-    )
-    middle = base + plain_product(attended, w_proj) + parts[4]
-    second = layer_norm(middle, parts[5], parts[6]).astype(jnp.bfloat16)
-    upward = plain_product(second, w_up) + parts[7]
-    activated = jax.nn.gelu(upward, approximate=False).astype(jnp.bfloat16)
-    result = middle + plain_product(activated, w_down) + parts[8]
-    saved = (
-        parts,
-        base,
-        normed,
-        query,
-        keys,
-        values,
-        soft,
-        attended,
-        middle,
-        second,
-        upward,
-        activated,
-    )
-    return (result, saved)
-
-
-def block_backward(saved, grad_grid, weights, onehot):
-    batch, rows, cols, _ = grad_grid.shape
-    w_qkv, w_proj, w_up, w_down = weights
-    parts, base, normed, query, keys, values, soft, attended, middle, second, upward, activated = (
-        saved
-    )
-    grad_out = to_windows(grad_grid).reshape(-1, D)
-    down_in = grad_out.astype(jnp.bfloat16)
-    grad_down = left_product(activated, down_in)
-    grad_act = right_product(down_in, w_down)
-    _, gelu_back = jax.vjp(lambda inner: jax.nn.gelu(inner, approximate=False), upward)
-    grad_up = gelu_back(grad_act)[0]
-    up_in = grad_up.astype(jnp.bfloat16)
-    grad_upw = left_product(second, up_in)
-    grad_second = right_product(up_in, w_up)
-    _, second_back = jax.vjp(layer_norm, middle, parts[5], parts[6])
-    grad_mid_norm, grad_gain2, grad_bias2 = second_back(grad_second)
-    grad_mid = grad_out + grad_mid_norm
-    proj_in = grad_mid.astype(jnp.bfloat16)
-    grad_proj = left_product(attended, proj_in)
-    grad_att = right_product(proj_in, w_proj).astype(jnp.bfloat16).reshape(-1, WIN * WIN, H, HD)
-    grad_soft = batched("wihd,wjhd->whij", grad_att, values)
-    grad_values = batched("whij,wihd->wjhd", soft.astype(jnp.bfloat16), grad_att)
-    grad_scores = soft * (grad_soft - jnp.sum(soft * grad_soft, -1, keepdims=True))
-    pair_sums = jnp.sum(grad_scores, 0).transpose(1, 2, 0).reshape(-1, grad_scores.shape[1])
-    grad_table = lax.dot_general(
-        onehot, pair_sums, (((0,), (0,)), ((), ())), precision=lax.Precision.HIGHEST
-    )
-    scores_b = grad_scores.astype(jnp.bfloat16)
-    grad_query = (batched("whij,wjhd->wihd", scores_b, keys) * HD ** (-0.5)).reshape(-1, D)
-    grad_keys = batched("whij,wihd->wjhd", scores_b, query).reshape(-1, D)
-    grad_values = grad_values.reshape(-1, D)
-    mixed_in = jnp.concatenate([grad_query, grad_keys, grad_values], 1).astype(jnp.bfloat16)
-    grad_qkv = left_product(normed, mixed_in)
-    grad_normed = right_product(mixed_in, w_qkv)
-    _, first_back = jax.vjp(layer_norm, base, parts[0], parts[1])
-    grad_base_norm, grad_gain1, grad_bias1 = first_back(grad_normed)
-    grad_base = grad_mid + grad_base_norm
-    grad_vectors = jnp.concatenate(
-        [
-            grad_gain1,
-            grad_bias1,
-            jnp.sum(grad_query, 0),
-            jnp.sum(grad_values, 0),
-            jnp.sum(grad_mid, 0),
-            grad_gain2,
-            grad_bias2,
-            jnp.sum(grad_up, 0),
-            jnp.sum(grad_out, 0),
-        ]
-    )
-    grid_out = from_windows(grad_base.reshape(-1, WIN * WIN, D), batch, rows, cols)
-    return (grid_out, (grad_qkv, grad_proj, grad_upw, grad_down, grad_vectors), grad_table)
+        bias = jnp.where(allowed[:, None], bias, FAR)
+    short = PADDED - WIN * WIN
+    bias = jnp.pad(bias, ((0, 0), (0, 0), (0, short), (0, 0)))
+    bias = jnp.pad(bias, ((0, 0), (0, 0), (0, 0), (0, short)), constant_values=FAR)
+    return bias.reshape(bias.shape[0], D // LANES, -1, PADDED)
+
+
+def table_sums(dscore, onehot):
+    sums = dscore.reshape(H, PADDED, PADDED)[:, : WIN * WIN, : WIN * WIN]
+    sums = sums.transpose(1, 2, 0).reshape(-1, H)
+    return lax.dot_general(
+        onehot, sums, (((0,), (0,)), ((), ())), precision=lax.Precision.HIGHEST
+    )
+
+
+def regroup(packed, share):
+    if share % 16 == 0:
+        return packed
+    owners = packed.shape[0]
+    pieces = [packed[:, cols(c, share)].reshape(1, D, D) for c in range(8)]
+    pieces.append(packed[:, 8 * share : 12 * share].reshape(1, FF, D))
+    return jnp.concatenate(pieces, 1)
+
+
+def ungroup(whole, owners):
+    if whole.shape[0] == owners:
+        return whole
+    pieces = [whole[0, cols(c)].reshape(owners, -1, D) for c in range(8)]
+    pieces.append(whole[0, 8 * D :].reshape(owners, -1, D))
+    return jnp.concatenate(pieces, 1)
 
 
 MESH_IDS = pl.DeviceIdType.MESH
@@ -327,7 +466,8 @@
 
 def scatter_kernel(
     count,
-    parts,
+    part0,
+    part1,
     out,
     mine,
     theirs,
@@ -349,8 +489,9 @@
     behind = ring_index(place - 1, count)
     ups = count // 2
     downs = count - 1 - ups
-    keep = pltpu.make_async_copy(parts.at[section], mine, local_sem)
-    keep.start()
+    keep = [pltpu.make_async_copy(part, mine, local_sem) for part in (part0, part1)]
+    pl.when(section == 0)(keep[0].start)
+    pl.when(section == 1)(keep[1].start)
     enter(section, me, ahead, behind)
     offsets = []
     for step in range(ups):
@@ -361,16 +502,20 @@
     sides = {}
     for slot, offset in enumerate(offsets):
         block = ring_index(place + offset, count)
-        side = remote(
-            parts.at[1 - section, block],
-            theirs.at[block],
-            side_s.at[slot],
-            side_r.at[slot],
-            (1 - section, me),
-        )
-        side.start()
-        sides[offset] = side
-    keep.wait()
+        pair = [
+            remote(
+                part.at[block],
+                theirs.at[block],
+                side_s.at[slot],
+                side_r.at[slot],
+                (1 - section, me),
+            )
+            for part in (part0, part1)
+        ]
+        pl.when(section == 0)(pair[1].start)
+        pl.when(section == 1)(pair[0].start)
+        sides[offset] = pair[0]
+    keep[0].wait()
 
     def local(offset):
         sides[offset].wait_recv()
@@ -416,15 +561,15 @@
         side.wait_send()
 
 
-def scatter_all(parts, count):
+def scatter_all(part0, part1, count):
     ups = count // 2
     downs = count - 1 - ups
-    block = parts.shape[2:]
-    kind = parts.dtype
+    block = part0.shape[1:]
+    kind = part0.dtype
     return pl.pallas_call(
         lambda *refs: scatter_kernel(count, *refs),
         out_shape=jax.ShapeDtypeStruct(block, jnp.float32),
-        in_specs=[pl.BlockSpec(memory_space=pl.ANY)],
+        in_specs=[pl.BlockSpec(memory_space=pl.ANY)] * 2,
         out_specs=pl.BlockSpec(memory_space=pltpu.VMEM),
         scratch_shapes=[
             pltpu.VMEM((count,) + block, kind),
@@ -442,7 +587,7 @@
         ],
         compiler_params=pltpu.CompilerParams(collective_id=1, has_side_effects=True),
         name="scatter_grads",
-    )(parts)
+    )(part0, part1)
 
 
 EXTRA = 16
@@ -458,16 +603,16 @@
     return jnp.concatenate(pieces + [row], 1).reshape(owners, -1, D)
 
 
-def unpack(packed, share, down_share, width):
+def unpack(packed, share):
     start = 0
     matrices = []
-    for extent, rows in ((3 * D, share), (D, share), (FF, share), (D, down_share)):
+    for extent, rows in ((3 * D, share), (D, share), (FF, share), (D, 4 * share)):
         pieces = []
         for _ in range(extent // D):
-            pieces.append(packed[:, start : start + rows])
+            pieces.append(packed[start : start + rows])
             start = start + rows
-        matrices.append(jnp.concatenate(pieces, 2).reshape(-1, extent))
-    return matrices, packed[:, start, :width].reshape(-1)
+        matrices.append(jnp.concatenate(pieces, 1))
+    return matrices
 
 
 def by_flag(flag, first, second):
@@ -507,7 +652,6 @@
     count = lax.axis_size("fsdp")
     groups = block_input.shape[1]
     share = qkv_weight.shape[1]
-    down_share = fc2_weight.shape[1]
     width = vectors.shape[1]
     onehot = relative_onehot()
     gathered = gather_all(
@@ -515,36 +659,35 @@
     )
     images = whole_images(jnp.stack([block_input, cotangent]), section, half)
     tables = by_flag(section, rel_table[0], swap_sections(rel_table[0]))
-    layers = [unpack(gathered[layer], share, down_share, width) for layer in range(2)]
-    masks = (None, allowed_pairs())
-
-    def forward(grid, layer):
-        weights, row = layers[layer]
-        result, saved = recompute(grid, weights, row, tables[layer], masks[layer], onehot)
-        batch = grid.shape[0]
-        out = from_windows(result.reshape(-1, WIN * WIN, D).astype(jnp.bfloat16), batch, SIDE, SIDE)
-        return out, saved
-
-    first_out, first_saved = forward(images[0], 0)
-    second_out, second_saved = forward(jnp.roll(first_out, (-SHIFT, -SHIFT), (1, 2)), 1)
-    second_out = jnp.roll(second_out, (SHIFT, SHIFT), (1, 2))
-    grad = jnp.roll(images[1], (-SHIFT, -SHIFT), (1, 2)).astype(jnp.float32)
-    second_grid, second_grads, second_table = block_backward(
-        second_saved, grad, layers[1][0], onehot
-    )
-    second_grid = jnp.roll(second_grid, (SHIFT, SHIFT), (1, 2))
-    first_grid, first_grads, first_table = block_backward(
-        first_saved, second_grid, layers[0][0], onehot
-    )
-
-    def owners(grads):
-        shaped = [piece.reshape(count, -1, piece.shape[-1]) for piece in grads[:4]]
-        return pack(*shaped, grads[4].reshape(count, -1)).astype(jnp.bfloat16)
-
-    summed = scatter_all(jnp.stack([owners(first_grads), owners(second_grads)]), count)
-    mine, row = unpack(summed[None], share, down_share, width)
-    table_total = lax.psum(jnp.stack([first_table, second_table]), ("section", "fsdp"))
-    table_total = jnp.where(section == 0, table_total[0], table_total[1])
+    biases = (
+        score_bias(tables[0], None, onehot),
+        score_bias(tables[1], allowed_pairs(), onehot),
+    )
+    grouped = [regroup(gathered[layer], share) for layer in range(2)]
+    rows = gathered[:, :, BLOCKS * share, :width].reshape(2, BLOCKS, D).astype(jnp.float32)
+    batch = images.shape[1]
+    inputs = [pad_windows(images[0])]
+    result = run_forward(inputs[0], grouped[0], rows[0], biases[0])
+    first_out, first_saved = unpad_windows(result[0], batch), result[1:]
+    inputs.append(pad_windows(jnp.roll(first_out, (-SHIFT, -SHIFT), (1, 2))))
+    result = run_forward(inputs[1], grouped[1], rows[1], biases[1])
+    second_saved = result[1:]
+    second_out = jnp.roll(unpad_windows(result[0], batch), (SHIFT, SHIFT), (1, 2))
+    grad = pad_windows(jnp.roll(images[1], (-SHIFT, -SHIFT), (1, 2)).astype(jnp.float32))
+    second = run_backward(grad, inputs[1], grouped[1], rows[1], second_saved)
+    second_grid = jnp.roll(unpad_windows(second[0], batch), (SHIFT, SHIFT), (1, 2))
+    first = run_backward(pad_windows(second_grid), inputs[0], grouped[0], rows[0], first_saved)
+    first_grid = unpad_windows(first[0], batch)
+    summed = scatter_all(ungroup(first[1], count), ungroup(second[1], count), count)
+    mine = unpack(summed, share)
+    pair = [
+        jnp.concatenate([part[2].reshape(-1), table_sums(part[3], onehot).reshape(-1)])
+        for part in (first, second)
+    ]
+    small = lax.psum(jnp.stack(pair), ("section", "fsdp"))
+    small = jnp.where(section == 0, small[0], small[1])
+    row = lax.dynamic_slice_in_dim(small, lax.axis_index("fsdp") * width, width)
+    table_total = small[BLOCKS * D :].reshape(rel_table.shape[1:])
     produced = spread_images(first_out, second_out, section, half, groups)
     returned = spread_images(
         first_grid.astype(jnp.bfloat16), second_grid.astype(jnp.bfloat16), section, half, groups

time: 597 us -> 430 us (0.72)
  local copies, waits for them, and re-layouts: 218 us -> 42.3 us
  waiting for transfers between devices: 0.02 us -> 120 us
  matrix products: 84.4 us -> 7.74 us
  other arithmetic: 67.8 us -> 19.1 us
  Pallas kernels: 171 us -> 216 us
  blocking collectives: 38.9 us -> 0 us
  between operations: 3.1 us -> 15.2 us
    psum x0 -> x1, waiting for transfers between devices: none -> 116 us  [on_device(): small = lax.psum(jnp.stack(pair), ('section', 'fsdp'))]
    reshape x32 -> x15, local copies, waits for them, and re-layouts: 71.9 us -> 1.54 us  [the longest x6 0.87 us: from_windows(): tokens = tokens.reshape(batch, rows // WIN, cols // WIN, WIN, WIN, width)]
    dot_general x38 -> x4, matrix products: 76.7 us -> 7.74 us  [the longest x2 3.94 us: score_bias(): bias = jnp.dot(onehot, table, precision=lax.Precision.HIGHEST)]
    pallas_call x0 -> x4, Pallas kernels: none -> 53.7 us  [the longest x2 35 us: run_backward(): pl.pallas_call(backward_kernel, out_shape=shapes, in_specs=in_vmem(4 + le...]
    psum x1 -> x0, blocking collectives: 38.9 us -> none  [on_device(): lax.psum(jnp.stack([first_table, second_table]), ('section', 'fsdp'))]
    unnamed x353 -> x38, local copies, waits for them, and re-layouts: 30.7 us -> 8.37 us
    reduce_sum x21 -> x0, other arithmetic: 18.5 us -> none  [the longest x5 4.03 us: block_backward(): jnp.sum(grad_out, 0)]
    slice x20 -> x16, local copies, waits for them, and re-layouts: 22.3 us -> 7.04 us  [the longest x4 4.01 us: unpad_windows(): rows.reshape(-1, PADDED, D)[:, :WIN * WIN]]
  transfers between devices with their start and end apart: 6 -> 7, of which waited for: 0 -> 3; matrix products, arithmetic and copies ran while one was open for 17% -> 11% of each run, Pallas kernels for 29% -> 20%
where the time goes in v2:
time: 430 us; the launch traced here: 426 us
  Pallas kernels  216 us (50%)
  waiting for transfers between devices  120 us (28%)
  local copies, waits for them, and re-layouts  42.3 us (10%)
  other arithmetic  19.1 us (4%)
  between operations  15.2 us (4%)
  matrix products  7.74 us (2%)
  starting transfers between devices  5.74 us (1%)
    psum x1, waiting for transfers between devices, on_device(): small = lax.psum(jnp.stack(pair), ('section', 'fsdp'))  116 us
    pallas_call x1, Pallas kernels, gather_all(): pl.pallas_call(lambda *refs: gather_kernel(count, *refs), out_shape=jax.S...  83.8 us
    pallas_call x1, Pallas kernels, scatter_all(): pl.pallas_call(lambda *refs: scatter_kernel(count, *refs), out_shape=jax....  79 us
    pallas_call x2, Pallas kernels, run_backward(): pl.pallas_call(backward_kernel, out_shape=shapes, in_specs=in_vmem(4 + le...  35 us
    pallas_call x2, Pallas kernels, run_forward(): pl.pallas_call(forward_kernel, out_shape=shapes, in_specs=in_vmem(4), out...  18.7 us
    squeeze x1, local copies, waits for them, and re-layouts, on_device(): grouped = [regroup(gathered[layer], share) for layer in range(2)]  10.9 us
  transfers between devices with their start and end apart: 7, of which 3 were waited for; matrix products, arithmetic and copies ran while one was open for 11% of the time, Pallas kernels for 20%

profile of v2, /device:TPU:0, one launch (start us, length us, event | category | flops | bytes accessed | tf_op | source)
XLA Modules:
  0.0 426.2 jit_solution(6484304669849981862)
XLA Ops:
  7.3 2.4 fusion.20
  9.7 3.0 collective-permute-start
  19.6 83.8 %gather_weights.1 = bf16[2,16,400,512]{3,2,1,0:T(8,128)(2,1)} custom-call(bf16[400,512]{1,0:T(8,128)(2,1)} %bitcast.163), custom_call_target="tpu_custom_call" | custom-call | tf_op jit(solution)/shard_map/gather_weights/pallas_call | solution.py:448
  103.4 10.9 %slice_bitcast_fusion = (bf16[16,400,512]{2,1,0:T(8,128)(2,1)}, bf16[16,400,512]{2,1,0:T(8,128)(2,1)}) fusion(bf16[2,16,400,512]{3,2,1,0:T(8,128)(2,1)} %gather_weights.1), kind=kLoop, calls=%fused_computation | loop fusion | bytes 26214400 | tf_op jit(solution)/shard_map/squeeze | solution.py:666
  117.4 2.0 fusion.14
  119.4 2.0 fusion.1
  122.6 1.6 pad_select_fusion
  126.7 9.0 %layer_forward.2 = (bf16[256,512]{1,0:T(8,128)(2,1)}, bf16[256,512]{1,0:T(8,128)(2,1)}, bf16[256,1536]{1,0:T(8,128)(2,1)}, f32[16,256,64]{2,1,0:T(8,128)}, bf16[...) custom-call(bf16[256,512]{1,0:T(8,128)(2,1)} %bitcast.138, ...), custom_call_target="tpu_custom_call" | custom-call | tf_op jit(solution)/shard_map/layer_forward/pallas_call | solution.py:268
  138.1 9.7 %layer_forward.3 = (bf16[256,512]{1,0:T(8,128)(2,1)}, bf16[256,512]{1,0:T(8,128)(2,1)}, bf16[256,1536]{1,0:T(8,128)(2,1)}, f32[16,256,64]{2,1,0:T(8,128)}, bf16[...) custom-call(bf16[256,512]{1,0:T(8,128)(2,1)} %bitcast.140, ...), custom_call_target="tpu_custom_call" | custom-call | tf_op jit(solution)/shard_map/layer_forward/pallas_call | solution.py:268
  151.7 17.5 %layer_backward.2 = (f32[256,512]{1,0:T(8,128)}, bf16[16,384,512]{2,1,0:T(8,128)(2,1)}, f32[12,512]{1,0:T(8,128)}, f32[4,256,64]{2,1,0:T(8,128)}) custom-call(f32[256,512]{1,0:T(8,128)} %bitcast_convert_fusion.grad, bf16[256,512]{1,0:T(8,128)(2,1)} %bitcast.141, bf16[16,400,512]{2,1,0:T(8,128)(2,1)} %get-tuple-element.106.w, f32[12,512]{1,0:T(8,128)} %squeeze.45.vec, ...), custom_call_target="tpu_custom_call" | custom-call | tf_op jit(solution)/shard_map/layer_backward/pallas_call | solution.py:287
  173.2 17.5 %layer_backward.3 = (f32[256,512]{1,0:T(8,128)}, bf16[16,384,512]{2,1,0:T(8,128)(2,1)}, f32[12,512]{1,0:T(8,128)}, f32[4,256,64]{2,1,0:T(8,128)}) custom-call(f32[256,512]{1,0:T(8,128)} %bitcast.143, bf16[256,512]{1,0:T(8,128)(2,1)} %bitcast.139, bf16[16,400,512]{2,1,0:T(8,128)(2,1)} %get-tuple-element.107.w, f32[12,512]{1,0:T(8,128)} %squeeze.20.vec, ...), custom_call_target="tpu_custom_call" | custom-call | tf_op jit(solution)/shard_map/layer_backward/pallas_call | solution.py:287
  192.2 79.0 %scatter_grads.1 = f32[384,512]{1,0:T(8,128)} custom-call(bf16[16,384,512]{2,1,0:T(8,128)(2,1)} %get-tuple-element.54.refs_0_, bf16[16,384,512]{2,1,0:T(8,128)(2,1)} %get-tuple-element.55.refs_1_), custom_call_target="tpu_custom_call" | custom-call | tf_op jit(solution)/shard_map/scatter_grads/pallas_call | solution.py:569
  271.3 1.8 fusion.32
  273.1 1.7 slice_bitcast_fusion.4
  276.8 1.9 fusion.6
  279.1 1.9 fusion.8
  284.6 115.6 %all-reduce.11.cloned.1.call-done = f32[2,8848]{1,0:T(2,128)} async-done(((f32[2,8848]{1,0:T(2,128)}), f32[2,8848]{1,0:T(2,128)}) %all-reduce.11.cloned.1.call-update) | async-done | bytes 70800 | tf_op jit(solution)/shard_map/psum | solution.py:687
  401.2 1.1 copy.211
  402.6 1.8 broadcast_select_fusion.2
  404.7 1.5 collective-permute-start.3
  406.7 1.8 broadcast_select_fusion.1
  411.0 1.6 collective-permute-done.3
  414.5 2.5 collective-permute-done.5
  417.4 1.7 copy.237
  (158 shorter events, 37.8 us)
Async XLA Ops:
  7.2 11.6 %copy-start.4 = (bf16[1,128,512]{2,1,0:T(8,128)(2,1)S(1)}, bf16[1,128,512]{2,1,0:T(8,128)(2,1)}, u32[]{:S(2)}) copy-start(bf16[1,128,512]{2,1,0:T(8,128)(2,1)} %param.13) | copy-start | bytes 393220
  7.2 11.6 %copy-start.8 = (bf16[1,384]{1,0:T(2,128)(2,1)S(1)}, bf16[1,384]{1,0:T(2,128)(2,1)}, u32[]{:S(2)}) copy-start(bf16[1,384]{1,0:T(2,128)(2,1)} %param.14) | copy-start | bytes 2308
  7.2 393.0 %all-reduce.11.cloned.1.call-start = ((), (), s32[]{:S(2)}) async-start(), calls=%async_computation | async-start | bytes 143360 | tf_op jit(solution)/shard_map/psum | solution.py:687
  9.7 114.6 %collective-permute-start = (bf16[2,1,1,7,14,512]{5,1,4,3,2,0:T(2,128)(2,1)S(1)}, bf16[2,1,1,7,14,512]{5,1,4,3,2,0:T(2,128)(2,1)S(1)}, u32[]{:S(2)}, u32[]{:S(2)}) collective-permute-start(bf16[2,1,1,7,14,512]{5,1,4,3,2,0:T(2,128)(2,1)S(1)} %get-tuple-element.109), channel_id=1, source_target_pairs={{0,1},{1,0},{2,3},{3,2},{4,5},{5,4},{6,7},{7,6},{8,9},{9,8},{10,11... | collective-permute-start | bytes 602120 | tf_op jit(solution)/shard_map/ppermute | solution.py:22
  12.7 104.7 %collective-permute-start.1 = (f32[169,16]{0,1:T(8,128)}, f32[169,16]{0,1:T(8,128)S(1)}, u32[]{:S(2)}, u32[]{:S(2)}) collective-permute-start(f32[169,16]{0,1:T(8,128)} %bitcast.174), channel_id=1, source_target_pairs={{0,16},{16,0},{1,17},{17,1},{2,18},{18,2},{3,19},{19,3},{4,20},{20... | collective-permute-start | bytes 32456 | tf_op jit(solution)/shard_map/ppermute | solution.py:623
  18.8 0.8 copy-start
  103.4 14.0 %copy-start.7 = (f32[1,169,16]{1,2,0:T(8,128)S(1)}, f32[1,169,16]{1,2,0:T(8,128)}, u32[]{:S(2)}) copy-start(f32[1,169,16]{1,2,0:T(8,128)} %param.15) | copy-start | bytes 32452
  271.3 5.3 %copy-start.1 = (f32[4,256,64]{2,1,0:T(8,128)S(1)}, f32[4,256,64]{2,1,0:T(8,128)}, u32[]{:S(2)}) copy-start(f32[4,256,64]{2,1,0:T(8,128)} %get-tuple-element.59) | copy-start | bytes 786436
  274.7 126.5 %collective-permute-start.2 = (bf16[1,14,14,512]{3,1,2,0:T(8,128)(2,1)}, bf16[1,14,14,512]{3,1,2,0:T(8,128)(2,1)}, u32[]{:S(2)}, u32[]{:S(2)}) collective-permute-start(bf16[1,14,14,512]{3,1,2,0:T(8,128)(2,1)} %maximum_select_fusion), channel_id=1, source_target_pairs={{0,16},{16,0},{1,17},{17,1},{2,18},{18,2},{3,19},{19,3},{4,20},{20... | collective-permute-start | bytes 602120 | tf_op jit(solution)/shard_map/ppermute | solution.py:623
  275.0 3.8 copy-start.5
  275.8 3.1 copy-start.2
  275.8 130.5 %collective-permute-start.4 = (bf16[1,14,14,512]{3,1,2,0:T(8,128)(2,1)}, bf16[1,14,14,512]{3,1,2,0:T(8,128)(2,1)S(1)}, u32[]{:S(2)}, u32[]{:S(2)}) collective-permute-start(bf16[1,14,14,512]{3,1,2,0:T(8,128)(2,1)} %convert_select_fusion), channel_id=1, source_target_pairs={{0,16},{16,0},{1,17},{17,1},{2,18},{18,2},{3,19},{19,3},{4,20},{20... | collective-permute-start | bytes 602120 | tf_op jit(solution)/shard_map/ppermute | solution.py:623
  276.8 4.3 %copy-start.6 = (f32[12,512]{1,0:T(8,128)S(1)}, f32[12,512]{1,0:T(8,128)}, u32[]{:S(2)}) copy-start(f32[12,512]{1,0:T(8,128)} %get-tuple-element.56) | copy-start | bytes 73732
  278.9 4.3 %copy-start.3 = (f32[32,512]{1,0:T(8,128)S(1)}, f32[32,512]{1,0:T(8,128)}, u32[]{:S(2)}) copy-start(f32[32,512]{1,0:T(8,128)} %get-tuple-element.113) | copy-start | bytes 196612
  404.7 7.9 %collective-permute-start.3 = (bf16[2,1,1,7,14,512]{5,0,4,3,2,1:T(2,128)(2,1)S(1)}, bf16[2,1,1,7,14,512]{5,0,4,3,2,1:T(2,128)(2,1)S(1)}, u32[]{:S(2)}, u32[]{:S(2)}) collective-permute-start(bf16[2,1,1,7,14,512]{5,0,4,3,2,1:T(2,128)(2,1)S(1)} %get-tuple-element.123), channel_id=1, source_target_pairs={{0,1},{1,0},{2,3},{3,2},{4,5},{5,4},{6,7},{7,6},{8,9},{9,8},{10,11... | collective-permute-start | bytes 602120 | tf_op jit(solution)/shard_map/ppermute | solution.py:22
  409.0 7.9 %collective-permute-start.5 = (bf16[2,1,1,7,14,512]{5,0,4,3,2,1:T(2,128)(2,1)S(1)}, bf16[2,1,1,7,14,512]{5,0,4,3,2,1:T(2,128)(2,1)S(1)}, u32[]{:S(2)}, u32[]{:S(2)}) collective-permute-start(bf16[2,1,1,7,14,512]{5,0,4,3,2,1:T(2,128)(2,1)S(1)} %get-tuple-element.119), channel_id=1, source_target_pairs={{0,1},{1,0},{2,3},{3,2},{4,5},{5,4},{6,7},{7,6},{8,9},{9,8},{10,11... | collective-permute-start | bytes 602120 | tf_op jit(solution)/shard_map/ppermute | solution.py:22
Sparse Core Ops, SparseCore 0:
  282.0 118.0 all-reduce.10
